TPU v7x, 512 devices: a whole 4x4x16 slice. The times are simulated.
512 devices in a mesh: dom: 64 (over z_hi, x, y, core), lag: 8 (over z_lo).
Axes of the slice: x: 4, y: 4, z: 16 (z_hi: 2, z_lo: 8; z = z_hi * 8 + z_lo), core: 2. Of those that a mesh axis runs over, the one named last changes fastest.
Arguments:
- delayed_crowd_history: bfloat16 [8, 64, 2048, 128], P('lag', None, 'dom'), may hold values from -6 to 6
- predicted_crowd_array: bfloat16 [64, 2048, 128], P('lag', 'dom'), may hold values from -40 to 40
- probe_target_spot: int32 [1024, 256], P('dom'), may hold values from 0 to 255
- alive_probe_places: int32 [1024], P('dom'), may hold values from 64 to 256, as said below
- probed_heat_levels: float32 [1024, 256], P('dom'), may hold values from -6 to 6
- probe_reciprocal_spread: float32 [1024, 256], P('dom'), may hold values from 0.1 to 1.6
- decay_extent_squares: int32 [1024], P('dom'), may hold values from 16 to 32
Outputs:
- smoothed: bfloat16 [8, 64, 2048, 128], P('lag', None, 'dom')
Inputs may be any that keep to these rules, and one draw needn't show every extreme that they name: `alive_probe_places`: live observations of a patch occupy its first slots.
All inputs are finite; a program needn't handle non-finite values.
Results may differ from a plain program's by a relative error of at most 0.0062.
Values may be sent and summed in bfloat16 or wider, within the bound.
A program may use at most 64 MiB of HBM per device.

v0:
```python
import jax
import jax.numpy as jnp
from jax import lax
from jax.sharding import PartitionSpec as P

PATCH = 16
NS_STEPS = 4
REACH = 2


def padded_2(block, sides, width):
    for axis, dim in sides:
        count = lax.axis_size(axis)
        forward = [(i, i + 1) for i in range(count - 1)]
        backward = [(target, source) for source, target in forward]
        low = lax.ppermute(
            lax.slice_in_dim(block, block.shape[dim] - width, None, axis=dim), axis, forward
        )
        high = lax.ppermute(lax.slice_in_dim(block, 0, width, axis=dim), axis, backward)
        block = jnp.concatenate([low, block, high], axis=dim)
    return block


def inverse_root(gram_part, right_side):
    crowd_members_number = gram_part.shape[-1]
    identity = jnp.eye(crowd_members_number, dtype=jnp.float32)
    frobenius = jnp.sqrt(jnp.sum(gram_part * gram_part, axis=(1, 2)))
    bound_value = crowd_members_number - 1.0 + frobenius
    iterate = (gram_part + (crowd_members_number - 1.0) * identity) / bound_value[:, None, None]
    root_iter = jnp.broadcast_to(identity, gram_part.shape)
    for sweep_index in range(NS_STEPS):
        correction = 1.5 * identity - 0.5 * jnp.matmul(
            root_iter, iterate, precision=lax.Precision.HIGHEST
        )
        iterate = jnp.matmul(iterate, correction, precision=lax.Precision.HIGHEST)
        root_iter = jnp.matmul(correction, root_iter, precision=lax.Precision.HIGHEST)
    inner_prod = jnp.matmul(root_iter, right_side[:, :, None], precision=lax.Precision.HIGHEST)
    mean_weights = (
        jnp.matmul(root_iter, inner_prod, precision=lax.Precision.HIGHEST)[:, :, 0]
        / bound_value[:, None]
    )
    spread = jnp.sqrt(crowd_members_number - 1.0) / jnp.sqrt(bound_value)
    return (spread[:, None, None] * root_iter + mean_weights[:, :, None]).astype(jnp.bfloat16)


def local_gram(padded, radius, crowd_members_number, patch_rows, patch_cols):
    group_size = padded.shape[3]
    reach_width = 2 * REACH + 1
    col_base = jnp.repeat(
        (jnp.arange(reach_width, dtype=jnp.int32) - REACH) * PATCH, group_size
    ).astype(jnp.float32)
    gram_sum = jnp.zeros(
        (patch_rows, patch_cols, crowd_members_number, crowd_members_number), jnp.float32
    )
    right_side = jnp.zeros((patch_rows, patch_cols, crowd_members_number), jnp.float32)
    for shift_row in range(reach_width):
        pieces = [
            padded[:, shift_row : shift_row + patch_rows, shift_col : shift_col + patch_cols, :]
            for shift_col in range(reach_width)
        ]
        stacked = jnp.concatenate(pieces, axis=3)
        anomaly_near = stacked[:crowd_members_number]
        weight_near = stacked[crowd_members_number].astype(jnp.float32)
        innov_near = stacked[crowd_members_number + 1].astype(jnp.float32)
        row_offset = (
            (shift_row - REACH) * PATCH
            + stacked[crowd_members_number + 2].astype(jnp.float32)
            - 7.5
        )
        col_offset = col_base + stacked[crowd_members_number + 3].astype(jnp.float32) - 7.5
        taper_weight = jnp.square(
            jnp.maximum(
                0.0, 1.0 - (jnp.square(row_offset) + jnp.square(col_offset)) / jnp.square(radius)
            )
        )
        scaled = (taper_weight * weight_near * anomaly_near.astype(jnp.float32)).astype(
            jnp.bfloat16
        )
        weighted = (taper_weight * innov_near).astype(jnp.bfloat16)
        gram_sum = gram_sum + jnp.einsum(
            "mxyo,nxyo->xymn", scaled, anomaly_near, preferred_element_type=jnp.float32
        )
        right_side = right_side + jnp.einsum(
            "mxyo,xyo->xym", anomaly_near, weighted, preferred_element_type=jnp.float32
        )
    return (gram_sum, right_side)


def shards(
    delayed_crowd_history,
    predicted_crowd_array,
    probe_target_spot,
    alive_probe_places,
    probed_heat_levels,
    probe_reciprocal_spread,
    decay_extent_squares,
):
    lag_total = lax.axis_size("lag")
    lag_rank = lax.axis_index("lag")
    crowd_share_part, tile_vertical_extent, tile_lateral_extent = predicted_crowd_array.shape
    patch_rows = tile_vertical_extent // PATCH
    patch_cols = tile_lateral_extent // PATCH
    patch_total = patch_rows * patch_cols
    slot_count = probe_target_spot.shape[1]
    group_size = slot_count // lag_total
    index_patch = jnp.arange(patch_total, dtype=jnp.int32)
    lattice_node_place = (
        ((index_patch // patch_cols)[:, None] * PATCH + probe_target_spot // PATCH)
        * tile_lateral_extent
        + (index_patch % patch_cols)[:, None] * PATCH
        + probe_target_spot % PATCH
    )
    probed_markers = jnp.take(
        predicted_crowd_array.reshape(crowd_share_part, tile_vertical_extent * tile_lateral_extent),
        lattice_node_place.reshape(-1),
        axis=1,
    )
    probed_markers = probed_markers.reshape(crowd_share_part, patch_rows, patch_cols, slot_count)
    received = lax.all_to_all(probed_markers, "lag", split_axis=3, concat_axis=0, tiled=True)
    crowd_members_number = received.shape[0]
    average_reading = jnp.sum(received, axis=0, dtype=jnp.float32) / crowd_members_number
    obs_anomaly = (received.astype(jnp.float32) - average_reading).astype(jnp.bfloat16)
    slot_start = lag_rank * group_size

    def gather_fraction(table):
        piece = lax.dynamic_slice_in_dim(table, slot_start, group_size, 1)
        return piece.reshape(patch_rows, patch_cols, group_size)

    slot_index = slot_start + jnp.arange(group_size, dtype=jnp.int32)
    usable_entry = (slot_index[None, :] < alive_probe_places[:, None]).reshape(
        patch_rows, patch_cols, group_size
    )
    precision_share = gather_fraction(probe_reciprocal_spread)
    reading_fraction = gather_fraction(probed_heat_levels)
    cell_share = gather_fraction(probe_target_spot)
    obs_weight = jnp.where(usable_entry, precision_share, 0.0).astype(jnp.bfloat16)
    departure_vector = jnp.where(
        usable_entry, precision_share * (reading_fraction - average_reading), 0.0
    ).astype(jnp.bfloat16)
    placed = jnp.stack(
        [
            obs_weight,
            departure_vector,
            (cell_share // PATCH).astype(jnp.bfloat16),
            (cell_share % PATCH).astype(jnp.bfloat16),
        ],
        0,
    )
    combined = jnp.concatenate([obs_anomaly, placed], 0)
    extended = padded_2(combined, (("dom", 1),), REACH)
    padded = jnp.pad(extended, ((0, 0), (0, 0), (REACH, REACH), (0, 0)))
    radius = decay_extent_squares.reshape(patch_rows, patch_cols, 1).astype(jnp.float32)
    gram_sum, right_side = local_gram(padded, radius, crowd_members_number, patch_rows, patch_cols)
    gram_flat = gram_sum.reshape(patch_total, crowd_members_number, crowd_members_number)
    rhs_flat = right_side.reshape(patch_total, crowd_members_number)
    gram_all, rhs_all = lax.psum((gram_flat, rhs_flat), "lag")
    transform = inverse_root(gram_all, rhs_all)
    lag_state = delayed_crowd_history[0]
    lag_mean = jnp.sum(lag_state, axis=0, dtype=jnp.float32) / crowd_members_number
    lag_anomaly = (lag_state.astype(jnp.float32) - lag_mean).astype(jnp.bfloat16)
    patch_grid = lag_anomaly.reshape(crowd_members_number, patch_rows, PATCH, patch_cols, PATCH)
    mixing = transform.reshape(patch_rows, patch_cols, crowd_members_number, crowd_members_number)
    updated = jnp.einsum(
        "maibj,abmn->naibj", patch_grid, mixing, preferred_element_type=jnp.float32
    )
    result = (
        updated.reshape(crowd_members_number, tile_vertical_extent, tile_lateral_extent) + lag_mean
    )
    return result.astype(jnp.bfloat16)[None]


def solution(mesh):
    in_specs = (
        P("lag", None, "dom", None),
        P("lag", "dom", None),
        P("dom", None),
        P("dom"),
        P("dom", None),
        P("dom", None),
        P("dom"),
    )
    out_specs = P("lag", None, "dom", None)
    return jax.shard_map(shards, mesh=mesh, in_specs=in_specs, out_specs=out_specs, check_vma=False)
```

profile of v0, /device:TPU:2, one launch (start us, length us, event | category | flops | bytes accessed | tf_op | source)
XLA Modules:
  0.0 256.4 jit_solution(7928711825052308144)
XLA Ops:
  6.5 0.8 fusion.196
  7.3 0.8 fusion.195
  8.2 1.3 copy.242
  9.5 12.1 %gather_fusion = bf16[4096,8]{1,0:T(8,128)(2,1)S(1)} fusion(bf16[8,4096]{0,1:T(8,128)(2,1)S(1)} %bitcast.330, s32[4096]{0:T(1024)S(1)} %broadcast_clamp_fusion), kind=kCustom, calls=%fused_computation | custom fusion | bytes 147456 | tf_op jit(solution)/shard_map/jit(_take)/gather | solution.py:113
  21.6 1.5 copy.243
  23.6 1.0 fusion.165
  24.7 1.7 reshape.455
  26.4 12.5 %all-to-all-start = ((bf16[8,2,2048]{2,1,0:T(2,128)(2,1)}), bf16[8,2,2048]{2,1,0:T(2,128)(2,1)S(1)}, u32[]{:S(2)}, u32[]{:S(2)}) async-start(bf16[8,2,2048]{2,1,0:T(2,128)(2,1)} %reshape.455), calls=%async_computation | async-start | bytes 131072 | tf_op jit(solution)/shard_map/all_to_all | solution.py:119
  39.0 0.7 copy.263
  39.7 0.4 convert_reduce_fusion.1
  40.2 0.7 convert_element_type.329
  40.9 0.7 square.113
  41.7 0.6 fusion.39
  42.3 7.5 %all-to-all-done = bf16[8,2,2048]{2,1,0:T(2,128)(2,1)S(1)} async-done(((bf16[8,2,2048]{2,1,0:T(2,128)(2,1)}), bf16[8,2,2048]{2,1,0:T(2,128)(2,1)S(1)}, u32[]{:S(2)}, u32[]{:S(2)}) %all-to-all-start) | async-done | bytes 65568 | tf_op jit(solution)/shard_map/all_to_all | solution.py:119
  49.8 1.2 reshape.456
  51.0 2.0 convert_reduce_fusion
  53.3 1.0 copy.283
  54.7 1.9 collective-permute-start
  56.6 5.9 %collective-permute-start.1 = (bf16[68,2,8,32]{3,2,1,0:T(8,128)(2,1)S(1)}, bf16[68,2,8,32]{3,2,1,0:T(8,128)(2,1)S(1)}, u32[]{:S(2)}, u32[]{:S(2)}) collective-permute-start(bf16[68,2,8,32]{3,2,1,0:T(8,128)(2,1)S(1)} %constant_dynamic-update-slice_fusion), channel_id=1, source_target_pairs={{8,0},{16,8},{24,16},{32,24},{40,32},{48,40},{56,48},{64,56},{72,6... | collective-permute-start | bytes 208904 | tf_op jit(solution)/shard_map/ppermute | solution.py:19
  62.6 2.1 collective-permute-done
  64.7 1.8 collective-permute-done.1
  66.4 0.7 fusion.5
  67.2 2.7 %fusion.164 = (bf16[68,2,8,32]{3,2,1,0:T(8,128)(2,1)}, bf16[68,2,8,32]{3,2,1,0:T(8,128)(2,1)}, bf16[68,2,8,32]{3,2,1,0:T(8,128)(2,1)}, bf16[68,2,8,32]{3,2,1,0:T...) fusion(bf16[68,6,12,32]{3,2,1,0:T(8,128)(2,1)S(1)} %fusion.5), kind=kLoop, calls=%fused_computation.253 | loop fusion | bytes 2646016 | tf_op jit(solution)/shard_map/slice | solution.py:58
  70.1 0.8 copy.251
  70.9 0.8 copy.247
  71.7 0.8 copy.249
  72.5 1.6 concatenate.29
  74.1 0.7 slice_convert_fusion
  74.7 0.8 pad_maximum_fusion
  75.6 1.6 concatenate.31
  77.2 0.8 slice.215
  78.0 1.5 concatenate.32
  79.6 0.8 slice.223
  80.4 1.7 concatenate.34
  82.1 0.8 slice.231
  82.9 2.4 concatenate.35
  85.4 1.1 slice.239
  86.5 1.6 fusion.157
  88.1 0.8 fusion.21
  89.0 0.9 fusion.138
  90.5 0.4 fusion.17
  91.4 0.4 fusion.15
  92.5 0.4 convolution_add_fusion.1
  92.9 1.2 convolution_add_fusion
  94.2 1.3 fusion.23
  95.5 26.8 %psum.15 = f32[16,64]{1,0:T(8,128)S(1)} all-reduce(f32[16,64]{1,0:T(8,128)S(1)} %add_bitcast_fusion), channel_id=1, replica_groups=mesh['dom'=64,'lag'=8] {'lag'}, use_global_device_ids=true, to_apply=%region_4.5 | all-reduce | flops 1024 | bytes 8192 | tf_op jit(solution)/shard_map/psum | solution.py:156
  122.3 111.9 %all-reduce.3.cloned.1.call-done = f32[16,64,64]{2,1,0:T(8,128)} async-done(((f32[16,64,64]{2,1,0:T(8,128)}), f32[16,64,64]{2,1,0:T(8,128)}) %all-reduce.3.cloned.1.call-update) | async-done | bytes 262160 | tf_op jit(solution)/shard_map/psum | solution.py:156
  234.2 1.3 multiply_reduce_fusion
  235.5 1.7 fusion.9
  237.2 0.6 fusion.35
  237.8 0.7 fusion.38
  238.6 0.6 fusion.8
  239.2 0.6 fusion.167
  239.9 0.6 fusion.166
  240.5 0.6 fusion.7
  241.2 0.6 fusion.169
  241.8 0.6 fusion.168
  242.5 0.6 fusion.6
  243.1 0.6 fusion.170
  243.8 0.9 convolution_bitcast_fusion.1
  244.7 0.9 fusion.171
  246.0 0.9 convolution_bitcast_fusion
  247.2 0.7 add_convert_fusion
  247.9 1.6 copy.266
  (74 shorter events, 4.1 us)
Async XLA Ops:
  23.1 15.8 %copy-start.15 = (s32[16]{0:T(128)S(1)}, s32[16]{0:T(128)}, u32[]{:S(2)}) copy-start(s32[16]{0:T(128)} %param.13) | copy-start | bytes 196
  23.1 15.8 %copy-start.7 = (bf16[1,64,32,128]{3,2,1,0:T(8,128)(2,1)S(1)}, bf16[1,64,32,128]{3,2,1,0:T(8,128)(2,1)}, u32[]{:S(2)}) copy-start(bf16[1,64,32,128]{3,2,1,0:T(8,128)(2,1)} %param.7) | copy-start | bytes 1572868
  24.6 15.4 %copy-start.16 = (s32[16]{0:T(128)S(1)}, s32[16]{0:T(128)}, u32[]{:S(2)}) copy-start(s32[16]{0:T(128)} %param.10) | copy-start | bytes 196
  26.4 23.4 %all-to-all-start = ((bf16[8,2,2048]{2,1,0:T(2,128)(2,1)}), bf16[8,2,2048]{2,1,0:T(2,128)(2,1)S(1)}, u32[]{:S(2)}, u32[]{:S(2)}) async-start(bf16[8,2,2048]{2,1,0:T(2,128)(2,1)} %reshape.455), calls=%async_computation | async-start | bytes 131072 | tf_op jit(solution)/shard_map/all_to_all | solution.py:119
  38.9 195.3 %all-reduce.3.cloned.1.call-start = ((), (), s32[]{:S(2)}) async-start(), calls=%async_computation.1 | async-start | bytes 1048576 | tf_op jit(solution)/shard_map/psum | solution.py:156
  51.0 3.3 %copy-start.11 = (f32[16,256]{1,0:T(8,128)S(1)}, f32[16,256]{1,0:T(8,128)}, u32[]{:S(2)}) copy-start(f32[16,256]{1,0:T(8,128)} %param.12) | copy-start | bytes 49156
  51.0 3.4 %copy-start.14 = (f32[16,256]{1,0:T(8,128)S(1)}, f32[16,256]{1,0:T(8,128)}, u32[]{:S(2)}) copy-start(f32[16,256]{1,0:T(8,128)} %param.11) | copy-start | bytes 49156
  51.0 3.5 %copy-start.9 = (s32[16,256]{1,0:T(8,128)S(1)}, s32[16,256]{1,0:T(8,128)}, u32[]{:S(2)}) copy-start(s32[16,256]{1,0:T(8,128)} %param.9) | copy-start | bytes 49156
  54.7 10.0 %collective-permute-start = (bf16[68,2,8,32]{3,2,1,0:T(8,128)(2,1)S(1)}, bf16[68,2,8,32]{3,2,1,0:T(8,128)(2,1)S(1)}, u32[]{:S(2)}, u32[]{:S(2)}) collective-permute-start(bf16[68,2,8,32]{3,2,1,0:T(8,128)(2,1)S(1)} %constant_dynamic-update-slice_fusion), channel_id=1, source_target_pairs={{0,8},{8,16},{16,24},{24,32},{32,40},{40,48},{48,56},{56,64},{64,7... | collective-permute-start | bytes 208904 | tf_op jit(solution)/shard_map/ppermute | solution.py:16
  56.6 9.8 %collective-permute-start.1 = (bf16[68,2,8,32]{3,2,1,0:T(8,128)(2,1)S(1)}, bf16[68,2,8,32]{3,2,1,0:T(8,128)(2,1)S(1)}, u32[]{:S(2)}, u32[]{:S(2)}) collective-permute-start(bf16[68,2,8,32]{3,2,1,0:T(8,128)(2,1)S(1)} %constant_dynamic-update-slice_fusion), channel_id=1, source_target_pairs={{8,0},{16,8},{24,16},{32,24},{40,32},{48,40},{56,48},{64,56},{72,6... | collective-permute-start | bytes 208904 | tf_op jit(solution)/shard_map/ppermute | solution.py:19
  66.4 8.3 %copy-start.1 = (bf16[68,2,8,32]{3,2,1,0:T(8,128)(2,1)}, bf16[68,2,8,32]{3,2,1,0:T(8,128)(2,1)S(1)}, u32[]{:S(2)}) copy-start(bf16[68,2,8,32]{3,2,1,0:T(8,128)(2,1)S(1)} %collective-permute-done.1) | copy-start | bytes 208900
  74.7 3.3 %copy-start.6 = (bf16[68,2,8,32]{3,2,1,0:T(8,128)(2,1)S(1)}, bf16[68,2,8,32]{3,2,1,0:T(8,128)(2,1)}, u32[]{:S(2)}) copy-start(bf16[68,2,8,32]{3,2,1,0:T(8,128)(2,1)} %get-tuple-element.15) | copy-start | bytes 208900
  85.4 4.5 %copy-start = (bf16[68,2,8,160]{3,2,1,0:T(8,128)(2,1)S(1)}, bf16[68,2,8,160]{3,2,1,0:T(8,128)(2,1)}, u32[]{:S(2)}) copy-start(bf16[68,2,8,160]{3,2,1,0:T(8,128)(2,1)} %concatenate.35) | copy-start | bytes 1044484
  86.5 6.4 %copy-start.4 = (bf16[64,2,8,160]{3,2,1,0:T(8,128)(2,1)}, bf16[64,2,8,160]{3,2,1,0:T(8,128)(2,1)S(1)}, u32[]{:S(2)}) copy-start(bf16[64,2,8,160]{3,2,1,0:T(8,128)(2,1)S(1)} %slice.239) | copy-start | bytes 983044
  88.1 2.0 copy-start.3
  90.1 1.0 copy-start.2
  90.8 1.1 copy-start.5
  92.5 1.7 copy-start.12
  92.9 2.6 copy-start.13
  92.9 142.6 %copy-start.10 = (f32[64,64]{1,0:T(8,128)S(1)}, f32[64,64]{1,0:T(8,128)}, u32[]{:S(2)}) copy-start(f32[64,64]{1,0:T(8,128)} %get-tuple-element.46) | copy-start | bytes 49156
  234.2 3.6 %copy-start.8 = (f32[16,64,64]{2,1,0:T(8,128)S(1)}, f32[16,64,64]{2,1,0:T(8,128)}, u32[]{:S(2)}) copy-start(f32[16,64,64]{2,1,0:T(8,128)} %all-reduce.3.cloned.1.call-done) | copy-start | bytes 786436
Sparse Core Ops, SparseCore 0:
  94.3 139.8 all-reduce.2
where the time goes:
time: 257 us; the launch traced here: 256 us
  waiting for transfers between devices  123 us (48%)
  local copies, waits for them, and re-layouts  41.4 us (16%)
  blocking collectives  26.8 us (10%)
  starting transfers between devices  20.4 us (8%)
  matrix products  16.5 us (6%)
  other arithmetic  14 us (5%)
  between operations  14 us (5%)
    psum x1, waiting for transfers between devices, shards(): gram_all, rhs_all = lax.psum((gram_flat, rhs_flat), 'lag')  112 us
    psum x1, blocking collectives, shards(): gram_all, rhs_all = lax.psum((gram_flat, rhs_flat), 'lag')  26.8 us
    gather x2, local copies, waits for them, and re-layouts, shards(): jnp.take(predicted_crowd_array.reshape(crowd_share_part, tile_vertical_ex...  13.6 us
    all_to_all x1, starting transfers between devices, shards(): lax.all_to_all(probed_markers, 'lag', split_axis=3, concat_axis=0, tiled=...  12.5 us
    concatenate x5, local copies, waits for them, and re-layouts, local_gram(): stacked = jnp.concatenate(pieces, axis=3)  8.81 us
    all_to_all x1, waiting for transfers between devices, shards(): lax.all_to_all(probed_markers, 'lag', split_axis=3, concat_axis=0, tiled=...  7.52 us
    ppermute x1, starting transfers between devices, padded_2(): lax.ppermute(lax.slice_in_dim(block, 0, width, axis=dim), axis, backward)  5.93 us
    unnamed x39, local copies, waits for them, and re-layouts  5.35 us
  transfers between devices with their start and end apart: 4, of which 4 were waited for; matrix products, arithmetic and copies ran while one was open for 2% of the time, Pallas kernels for 0%

commit v1 on v0

v1 whole, which is shorter than its diff:
```python
import functools

import jax
import jax.numpy as jnp
from jax import lax
from jax.experimental import pallas as pl
from jax.experimental.pallas import tpu as pltpu
from jax.sharding import PartitionSpec as P

PATCH = 16
NS_STEPS = 4
HALO = 3
MESH = pl.DeviceIdType.MESH
NT = (((1,), (1,)), ((), ()))


def split2(x):
    high = x.astype(jnp.bfloat16)
    return high, (x - high.astype(jnp.float32)).astype(jnp.bfloat16)


def product(x, y):
    xh, xl = split2(x)
    yh, yl = split2(y)
    dot = functools.partial(jnp.dot, preferred_element_type=jnp.float32)
    return dot(xh, yh) + (dot(xh, yl) + dot(xl, yh))


def kernel(
    tiles,
    lags,
    fore_ref,
    spot_ref,
    heat_ref,
    spread_ref,
    alive_ref,
    radius_ref,
    hist_hbm,
    out_ref,
    hist_ref,
    lift_ref,
    mean_ref,
    turned_ref,
    fore32_ref,
    send_ref,
    cells_ref,
    field_ref,
    wsend_ref,
    wcells_ref,
    acc_ref,
    gsend_ref,
    gram_ref,
    rsend_ref,
    rhs_ref,
    tsend_ref,
    trans_ref,
    hist_sem,
    send_sem,
    recv_sem,
    wsend_sem,
    wrecv_sem,
    gsend_sem,
    grecv_sem,
    rsend_sem,
    rrecv_sem,
    tsend_sem,
    trecv_sem,
):
    tile = lax.axis_index("dom")
    lag = lax.axis_index("lag")
    share, rows, cols = fore_ref.shape
    members = share * lags
    groups = rows // lags
    patch_cols = cols // PATCH
    slots = spot_ref.shape[1]
    f32, bf16 = jnp.float32, jnp.bfloat16

    def place(target_tile, target_lag):
        return {"dom": target_tile, "lag": target_lag}

    def peer(step):
        return lax.rem(lag + step, lags)

    load = pltpu.make_async_copy(hist_hbm.at[0], hist_ref, hist_sem)
    load.start()

    barrier = pltpu.get_barrier_semaphore()

    def greet(target_tile, target_lag):
        pl.semaphore_signal(
            barrier, inc=1, device_id=place(target_tile, target_lag), device_id_type=MESH
        )

    @pl.loop(1, lags)
    def _(step):
        greet(tile, peer(step))

    @pl.when(tile > 0)
    def _():
        @pl.loop(0, lags)
        def _(step):
            greet(tile - 1, step)

    @pl.when(tile < tiles - 1)
    def _():
        @pl.loop(0, lags)
        def _(step):
            greet(tile + 1, step)

    for m in range(share):
        fore32_ref[m * rows : (m + 1) * rows, :] = fore_ref[m].astype(f32)
    for target in range(lags):
        for k in range(groups):
            row = k * lags + target
            send_ref[target, k] = fore32_ref[pl.ds(row, share, stride=rows), :].astype(bf16)

    field_ref[...] = jnp.zeros_like(field_ref)
    slot_index = lax.broadcasted_iota(jnp.int32, (1, slots), 1)
    row_iota = lax.broadcasted_iota(jnp.int32, (PATCH, slots), 0)
    col_iota = lax.broadcasted_iota(jnp.int32, (cols, slots), 0)

    @pl.loop(0, rows // PATCH)
    def _(a):
        @pl.loop(0, patch_cols)
        def _(b):
            p = a * patch_cols + b
            spot = spot_ref[pl.ds(p, 1), :]
            live = slot_index < alive_ref[p]
            spread = jnp.where(live, spread_ref[pl.ds(p, 1), :], 0.0)
            weight = spread.astype(bf16).astype(f32)
            level = spread * heat_ref[pl.ds(p, 1), :]
            parts = [weight]
            for value in (level, spread):
                for _ in range(3):
                    part = value.astype(bf16).astype(f32)
                    parts.append(part)
                    value = value - part
            in_row = row_iota == lax.shift_right_logical(spot, 4)
            in_col = col_iota == (spot & (PATCH - 1)) + b * PATCH
            left = jnp.concatenate([jnp.where(in_row, part, 0.0) for part in parts], axis=0)
            right = jnp.where(in_col, 1.0, 0.0).astype(bf16)
            sums = lax.dot_general(left.astype(bf16), right, NT, preferred_element_type=f32)
            base = pl.multiple_of(a * PATCH, PATCH)
            for q, chosen in enumerate(((0,), (3, 2, 1), (6, 5, 4))):
                total = field_ref[pl.ds(q * rows + base, PATCH), :]
                for c in chosen:
                    total = total + sums[c * PATCH : (c + 1) * PATCH]
                field_ref[pl.ds(q * rows + base, PATCH), :] = total

    for k in range(groups):
        mine = field_ref[pl.ds(k * lags + lag, 8, stride=rows), :]
        wsend_ref[k] = mine
        wcells_ref[HALO + k] = mine

    for k in range(groups):
        cells_ref[HALO + k, lag] = send_ref[lag, k]

    @pl.when(tile == 0)
    def _():
        cells_ref[0:HALO] = jnp.zeros((HALO, lags, share, cols), bf16)
        wcells_ref[0:HALO] = jnp.zeros((HALO, 8, cols), f32)

    @pl.when(tile == tiles - 1)
    def _():
        cells_ref[HALO + groups :] = jnp.zeros((HALO, lags, share, cols), bf16)
        wcells_ref[HALO + groups :] = jnp.zeros((HALO, 8, cols), f32)

    neighbours = (
        lags - 1 + jnp.where(tile > 0, lags, 0) + jnp.where(tile < tiles - 1, lags, 0)
    )
    pl.semaphore_wait(barrier, neighbours)

    def cell_copy(kind, target_lag, source_lag):
        first = 1 if kind == 1 else 0
        count = groups if kind == 0 else HALO
        start = (HALO, 0, HALO + groups)[kind]
        return pltpu.make_async_remote_copy(
            src_ref=send_ref.at[target_lag, pl.ds(first, count)],
            dst_ref=cells_ref.at[pl.ds(start, count), source_lag],
            send_sem=send_sem.at[kind, target_lag],
            recv_sem=recv_sem.at[kind, source_lag],
            device_id=place(tile + (0, 1, -1)[kind], target_lag),
            device_id_type=MESH,
        )

    def weight_copy(kind):
        first = 1 if kind == 1 else 0
        start = (HALO, 0, HALO + groups)[kind]
        return pltpu.make_async_remote_copy(
            src_ref=wsend_ref.at[pl.ds(first, HALO)],
            dst_ref=wcells_ref.at[pl.ds(start, HALO)],
            send_sem=wsend_sem.at[kind - 1],
            recv_sem=wrecv_sem.at[kind - 1],
            device_id=place(tile + (0, 1, -1)[kind], lag),
            device_id_type=MESH,
        )

    has_below = tile < tiles - 1
    has_above = tile > 0

    @pl.when(has_below)
    def _():
        @pl.loop(0, lags)
        def _(step):
            cell_copy(1, peer(step), lag).start()

        weight_copy(1).start()

    @pl.when(has_above)
    def _():
        @pl.loop(0, lags)
        def _(step):
            cell_copy(2, peer(step), lag).start()

        weight_copy(2).start()

    @pl.loop(1, lags)
    def _(step):
        cell_copy(0, peer(step), lag).start()

    load.wait()

    def lift(m, total):
        state = hist_ref[m].astype(f32)
        lift_ref[pl.ds(pl.multiple_of(m * rows, rows), rows), :] = state
        return total + state

    mean = lax.fori_loop(0, members, lift, jnp.zeros((rows, cols), f32)) / members
    mean_ref[...] = mean

    @pl.loop(0, rows)
    def _(r):
        state = lift_ref[pl.ds(r, members, stride=rows), :]
        turned_ref[r] = (state - mean_ref[pl.ds(r, 1), :]).astype(bf16)

    sub = lax.broadcasted_iota(jnp.int32, (patch_cols, cols), 0)
    lane = lax.broadcasted_iota(jnp.int32, (patch_cols, cols), 1)
    col_offset = (lane - PATCH * sub).astype(f32) - 7.5
    col_square = col_offset * col_offset
    squares = []
    for a in range(2):
        radius = jnp.zeros((patch_cols, cols), f32)
        for b in range(patch_cols):
            value = radius_ref[a * patch_cols + b].astype(f32)
            radius = jnp.where(sub == b, value, radius)
        squares.append(radius * radius)

    acc_ref[...] = jnp.zeros_like(acc_ref)

    for step in range(1, lags):
        cell_copy(0, lag, peer(step)).wait_recv()

    @pl.when(has_above)
    def _():
        @pl.loop(0, lags)
        def _(step):
            cell_copy(1, lag, step).wait_recv()

        weight_copy(1).wait_recv()

    @pl.when(has_below)
    def _():
        @pl.loop(0, lags)
        def _(step):
            cell_copy(2, lag, step).wait_recv()

        weight_copy(2).wait_recv()

    @pl.loop(0, groups + 2 * HALO - 2)
    def _(i):
        row_offset = (lags * i + lag).astype(f32) - 31.5
        lefts, rights = [], []
        for a in range(2):
            values = cells_ref[i + 2 * a].astype(f32).reshape(members, cols)
            average = jnp.sum(values, axis=0, keepdims=True) / members
            anomaly = (values - average).astype(bf16)
            wide = anomaly.astype(f32)
            table = wcells_ref[i + 2 * a]
            innovation = table[1:2] - table[2:3] * average
            taper = jnp.maximum(0.0, 1.0 - (row_offset * row_offset + col_square) / squares[a])
            taper = taper * taper
            scale = taper * table[0:1]
            pieces = [(wide * scale[b : b + 1]).astype(bf16) for b in range(patch_cols)]
            extra = jnp.concatenate([taper * innovation, jnp.zeros_like(taper)], axis=0)
            lefts.append(jnp.concatenate(pieces + [extra.astype(bf16)], axis=0))
            empty = jnp.zeros_like(anomaly)
            pair = [anomaly, empty] if a == 0 else [empty, anomaly]
            rights.append(jnp.concatenate(pair, axis=0))
        left = jnp.concatenate(lefts, axis=1)
        right = jnp.concatenate(rights, axis=1)
        acc_ref[...] += lax.dot_general(left, right, NT, preferred_element_type=f32)

    for b in range(lags):
        gsend_ref[b] = acc_ref[b * members : (b + 1) * members].astype(bf16)
        rsend_ref[b] = acc_ref[patch_cols * members + b : patch_cols * members + b + 1]

    def gram_copies(target_lag, source_lag):
        where = place(tile, target_lag)
        return (
            pltpu.make_async_remote_copy(
                src_ref=gsend_ref.at[target_lag],
                dst_ref=gram_ref.at[source_lag],
                send_sem=gsend_sem.at[target_lag],
                recv_sem=grecv_sem.at[source_lag],
                device_id=where,
                device_id_type=MESH,
            ),
            pltpu.make_async_remote_copy(
                src_ref=rsend_ref.at[target_lag],
                dst_ref=rhs_ref.at[source_lag],
                send_sem=rsend_sem.at[target_lag],
                recv_sem=rrecv_sem.at[source_lag],
                device_id=where,
                device_id_type=MESH,
            ),
        )

    @pl.loop(1, lags)
    def _(step):
        for copy in gram_copies(peer(step), lag):
            copy.start()

    gram_ref[lag] = gsend_ref[lag]
    rhs_ref[lag] = rsend_ref[lag]

    @pl.loop(1, lags)
    def _(step):
        for copy in gram_copies(lag, peer(step)):
            copy.wait_recv()

    gram = gram_ref[0].astype(f32)
    rhs = rhs_ref[0]
    for source in range(1, lags):
        gram = gram + gram_ref[source].astype(f32)
        rhs = rhs + rhs_ref[source]

    identity = (
        lax.broadcasted_iota(jnp.int32, (members, members), 0)
        == lax.broadcasted_iota(jnp.int32, (members, members), 1)
    ).astype(f32)
    halves = [gram[:, :members], gram[:, members:]]
    sides = [rhs[:, :members], rhs[:, members:]]
    bounds = [
        members - 1.0
        + jnp.sqrt(jnp.sum(jnp.sum(half * half, axis=1, keepdims=True), axis=0, keepdims=True))
        for half in halves
    ]
    iterates = [
        (half + (members - 1.0) * identity) / bound for half, bound in zip(halves, bounds)
    ]
    roots = [1.5 * identity - 0.5 * iterate for iterate in iterates]
    iterates = [product(iterate, root) for iterate, root in zip(iterates, roots)]
    for sweep in range(1, NS_STEPS):
        corrections = [
            1.5 * identity - 0.5 * product(root, iterate)
            for root, iterate in zip(roots, iterates)
        ]
        if sweep < NS_STEPS - 1:
            iterates = [product(y, c) for y, c in zip(iterates, corrections)]
        roots = [product(c, root) for c, root in zip(corrections, roots)]
    transforms = []
    for root, side, bound in zip(roots, sides, bounds):
        inner = jnp.sum(root * side, axis=1, keepdims=True)
        weights = jnp.sum(root * inner, axis=0, keepdims=True) / bound
        factor = jnp.sqrt(jnp.full_like(bound, members - 1.0)) / jnp.sqrt(bound)
        transforms.append(factor * root + weights)
    tsend_ref[...] = jnp.concatenate(transforms, axis=1).astype(bf16)

    def transform_copy(target_lag, source_lag):
        return pltpu.make_async_remote_copy(
            src_ref=tsend_ref,
            dst_ref=trans_ref.at[source_lag],
            send_sem=tsend_sem.at[target_lag],
            recv_sem=trecv_sem.at[source_lag],
            device_id=place(tile, target_lag),
            device_id_type=MESH,
        )

    @pl.loop(1, lags)
    def _(step):
        transform_copy(peer(step), lag).start()

    trans_ref[lag] = tsend_ref[...]

    @pl.loop(1, lags)
    def _(step):
        cell_copy(0, peer(step), lag).wait_send()
        for copy in gram_copies(peer(step), lag):
            copy.wait_send()

    @pl.when(has_below)
    def _():
        @pl.loop(0, lags)
        def _(step):
            cell_copy(1, step, lag).wait_send()

        weight_copy(1).wait_send()

    @pl.when(has_above)
    def _():
        @pl.loop(0, lags)
        def _(step):
            cell_copy(2, step, lag).wait_send()

        weight_copy(2).wait_send()

    @pl.loop(1, lags)
    def _(step):
        transform_copy(lag, peer(step)).wait_recv()

    transforms = trans_ref[...].reshape(lags * members, 2 * members)
    lane_patch = lax.broadcasted_iota(jnp.int32, (members, cols), 1) // PATCH
    half_rows = rows // 2

    @pl.loop(0, half_rows)
    def _(i):
        first, second = turned_ref[i], turned_ref[i + half_rows]
        empty = jnp.zeros_like(first)
        right = jnp.concatenate(
            [
                jnp.concatenate([first, empty], axis=1),
                jnp.concatenate([empty, second], axis=1),
            ],
            axis=0,
        )
        mixed = jnp.dot(transforms, right, preferred_element_type=f32)
        for a in range(2):
            value = mixed[:members, a * cols : (a + 1) * cols]
            for b in range(1, patch_cols):
                piece = mixed[b * members : (b + 1) * members, a * cols : (a + 1) * cols]
                value = jnp.where(lane_patch == b, piece, value)
            r = i + a * half_rows
            lift_ref[pl.ds(r, members, stride=rows), :] = value + mean_ref[pl.ds(r, 1), :]

    @pl.loop(0, members)
    def _(m):
        state = lift_ref[pl.ds(pl.multiple_of(m * rows, rows), rows), :]
        out_ref[0, m] = state.astype(bf16)

    @pl.loop(1, lags)
    def _(step):
        transform_copy(peer(step), lag).wait_send()


def solution(mesh):
    tiles, lags = mesh.shape["dom"], mesh.shape["lag"]

    def shards(history, forecast, spot, alive, heat, spread, radius):
        share, rows, cols = forecast.shape
        members = share * lags
        groups = rows // lags
        patch_cols = cols // PATCH
        window = groups + 2 * HALO
        f32, bf16, dma = jnp.float32, jnp.bfloat16, pltpu.SemaphoreType.DMA
        vmem = pl.BlockSpec(memory_space=pltpu.VMEM)
        smem = pl.BlockSpec(memory_space=pltpu.SMEM)
        return pl.pallas_call(
            functools.partial(kernel, tiles, lags),
            out_shape=jax.ShapeDtypeStruct(history.shape, history.dtype),
            in_specs=[vmem, vmem, vmem, vmem, smem, smem, pl.BlockSpec(memory_space=pl.ANY)],
            out_specs=vmem,
            scratch_shapes=[
                pltpu.VMEM((members, rows, cols), bf16),
                pltpu.VMEM((members * rows, cols), f32),
                pltpu.VMEM((rows, cols), f32),
                pltpu.VMEM((rows, members, cols), bf16),
                pltpu.VMEM((share * rows, cols), f32),
                pltpu.VMEM((lags, groups, share, cols), bf16),
                pltpu.VMEM((window, lags, share, cols), bf16),
                pltpu.VMEM((8 * rows, cols), f32),
                pltpu.VMEM((groups, 8, cols), f32),
                pltpu.VMEM((window, 8, cols), f32),
                pltpu.VMEM((patch_cols * members + 16, 2 * members), f32),
                pltpu.VMEM((lags, members, 2 * members), bf16),
                pltpu.VMEM((lags, members, 2 * members), bf16),
                pltpu.VMEM((lags, 1, 2 * members), f32),
                pltpu.VMEM((lags, 1, 2 * members), f32),
                pltpu.VMEM((members, 2 * members), bf16),
                pltpu.VMEM((lags, members, 2 * members), bf16),
                dma,
                dma((3, lags)),
                dma((3, lags)),
                dma((2,)),
                dma((2,)),
                dma((lags,)),
                dma((lags,)),
                dma((lags,)),
                dma((lags,)),
                dma((lags,)),
                dma((lags,)),
            ],
            compiler_params=pltpu.CompilerParams(collective_id=0, has_side_effects=True),
            name="smoother",
        )(forecast, spot, heat, spread, alive, radius, history)

    in_specs = (
        P("lag", None, "dom", None),
        P("lag", "dom", None),
        P("dom", None),
        P("dom"),
        P("dom", None),
        P("dom", None),
        P("dom"),
    )
    out_specs = P("lag", None, "dom", None)
    return jax.shard_map(shards, mesh=mesh, in_specs=in_specs, out_specs=out_specs, check_vma=False)
```

time: 257 us -> 49.3 us (0.19)
  the two profiles are of different devices: /device:TPU:2 before, /device:TPU:31 now
where the time goes in v1:
time: 49.3 us; the launch traced here: 49.1 us
  Pallas kernels  47.2 us (96%)
  local copies, waits for them, and re-layouts  1.87 us (4%)
    pallas_call x1, Pallas kernels, shards(): pl.pallas_call(functools.partial(kernel, tiles, lags), out_shape=jax.Shap...  47.2 us
    unnamed x1, local copies, waits for them, and re-layouts  1.87 us

profile of v1, /device:TPU:31, one launch (start us, length us, event | category | flops | bytes accessed | tf_op | source)
XLA Modules:
  0.0 49.1 jit_solution(6172531319282257506)
XLA Ops:
  0.0 47.2 %smoother.1 = bf16[1,64,32,128]{3,2,1,0:T(8,128)(2,1)} custom-call(bf16[8,32,128]{2,1,0:T(8,128)(2,1)} %fore_ref.1, s32[16,256]{1,0:T(8,128)} %spot_ref.1, f32[16,256]{1,0:T(8,128)} %heat_ref.1, f32[16,256]{1,0:T(8,128)} %spread_ref.1, s32[16]{0:T(128)} %alive_ref.1, s32[16]{0:T(128)} %radius_ref.1, bf16[1,64,32,128]{3,2,1,0:T(8,128)(2,1)} %hist_hbm.1), custom_call_target="tpu_custom_call" | custom-call | tf_op jit(solution)/shard_map/smoother/pallas_call | solution.py:457
  47.3 1.9 %copy.9 = bf16[1,64,32,128]{3,2,1,0:T(8,128)(2,1)} copy(bf16[1,64,32,128]{3,2,1,0:T(8,128)(2,1)} %smoother.1) | data formatting | bytes 1048576

commit v2 on v0

v2 whole, which is shorter than its diff:
```python
import functools

import jax
import jax.numpy as jnp
from jax import lax
from jax.experimental import pallas as pl
from jax.experimental.pallas import tpu as pltpu
from jax.sharding import PartitionSpec as P

PATCH = 16
NS_STEPS = 4
WORKERS = 4
HALO = 24 // WORKERS
MESH = pl.DeviceIdType.MESH
NT = (((1,), (1,)), ((), ()))


def split2(x):
    high = x.astype(jnp.bfloat16)
    return high, (x - high.astype(jnp.float32)).astype(jnp.bfloat16)


def product(x, y):
    xh, xl = split2(x)
    yh, yl = split2(y)
    dot = functools.partial(jnp.dot, preferred_element_type=jnp.float32)
    return dot(xh, yh) + (dot(xh, yl) + dot(xl, yh))


def kernel(
    tiles,
    lags,
    fore_hbm,
    spot_hbm,
    heat_hbm,
    spread_hbm,
    alive_hbm,
    radius_hbm,
    hist_hbm,
    out_ref,
    fore_ref,
    spot_ref,
    heat_ref,
    spread_ref,
    alive_ref,
    radius_ref,
    hist_ref,
    mixed_ref,
    turn_ref,
    mean_ref,
    turned_ref,
    fore32_ref,
    send_ref,
    cells_ref,
    field_ref,
    wsend_ref,
    wcells_ref,
    acc_ref,
    gsend_ref,
    gram_ref,
    rsend_ref,
    rhs_ref,
    tsend_ref,
    trans_ref,
    load_sem,
    send_sem,
    recv_sem,
    wsend_sem,
    wrecv_sem,
    gsend_sem,
    grecv_sem,
    rsend_sem,
    rrecv_sem,
    tsend_sem,
    trecv_sem,
):
    tile = lax.axis_index("dom")
    lag = lax.axis_index("lag")
    share, rows, cols = fore_ref.shape
    members = share * lags
    groups = rows // WORKERS
    patch_cols = cols // PATCH
    slots = spot_ref.shape[1]
    block_rows = members + 16
    first = lags // 2 - WORKERS // 2
    f32, bf16 = jnp.float32, jnp.bfloat16
    has_below = tile < tiles - 1
    has_above = tile > 0
    mine = lag - first
    is_worker = jnp.logical_and(mine >= 0, mine < WORKERS)

    def place(target_tile, target_lag):
        return {"dom": target_tile, "lag": target_lag}

    loads = [
        pltpu.make_async_copy(source, target, load_sem.at[n])
        for n, (source, target) in enumerate(
            (
                (fore_hbm, fore_ref),
                (alive_hbm, alive_ref),
                (radius_hbm, radius_ref),
                (spot_hbm, spot_ref),
                (spread_hbm, spread_ref),
                (heat_hbm, heat_ref),
                (hist_hbm.at[0], hist_ref),
            )
        )
    ]

    barrier = pltpu.get_barrier_semaphore()

    def greet(target_tile, target_lag):
        pl.semaphore_signal(
            barrier, inc=1, device_id=place(target_tile, target_lag), device_id_type=MESH
        )

    @pl.when(is_worker)
    def _():
        @pl.when(has_above)
        def _():
            for target in range(lags):
                greet(tile - 1, target)

        @pl.when(has_below)
        def _():
            for target in range(lags):
                greet(tile + 1, target)

        for step in range(1, lags):
            greet(tile, lax.rem(lag + step, lags))

    for load in loads:
        load.start()

    loads[0].wait()
    for m in range(share):
        fore32_ref[m * rows : (m + 1) * rows, :] = fore_ref[m].astype(f32)
    for target in range(WORKERS):
        for k in range(groups):
            row = k * WORKERS + target
            send_ref[target, k] = fore32_ref[pl.ds(row, share, stride=rows), :].astype(bf16)

    pl.semaphore_wait(
        barrier,
        WORKERS
        - jnp.where(is_worker, 1, 0)
        + jnp.where(has_above, WORKERS, 0)
        + jnp.where(has_below, WORKERS, 0),
    )

    def cell_copy(kind, worker, source_lag):
        begin = groups - HALO if kind == 1 else 0
        count = groups if kind == 0 else HALO
        start = (HALO, 0, HALO + groups)[kind]
        return pltpu.make_async_remote_copy(
            src_ref=send_ref.at[worker, pl.ds(begin, count)],
            dst_ref=cells_ref.at[pl.ds(start, count), source_lag],
            send_sem=send_sem.at[kind, worker],
            recv_sem=recv_sem.at[kind, source_lag],
            device_id=place(tile + (0, 1, -1)[kind], first + worker),
            device_id_type=MESH,
        )

    def weight_copy(kind):
        begin = groups - HALO if kind == 1 else 0
        start = (HALO, 0, HALO + groups)[kind]
        return pltpu.make_async_remote_copy(
            src_ref=wsend_ref.at[pl.ds(begin, HALO)],
            dst_ref=wcells_ref.at[pl.ds(start, HALO)],
            send_sem=wsend_sem.at[kind - 1],
            recv_sem=wrecv_sem.at[kind - 1],
            device_id=place(tile + (0, 1, -1)[kind], lag),
            device_id_type=MESH,
        )

    def order(step):
        return jnp.where(lag < lags // 2, WORKERS - 1 - step, step)

    @pl.when(has_below)
    def _():
        for step in range(WORKERS):
            cell_copy(1, order(step), lag).start()

    @pl.when(has_above)
    def _():
        for step in range(WORKERS):
            cell_copy(2, order(step), lag).start()

    for step in range(WORKERS):
        worker = order(step)

        @pl.when(worker != mine)
        def _():
            cell_copy(0, worker, lag).start()

    for load in loads[1:6]:
        load.wait()

    def sides(kind, source_lag):
        return cell_copy(kind, 0, source_lag)

    def gram_copies(worker, source):
        where = place(tile, first + worker)
        return (
            pltpu.make_async_remote_copy(
                src_ref=gsend_ref.at[worker],
                dst_ref=gram_ref.at[source],
                send_sem=gsend_sem.at[worker],
                recv_sem=grecv_sem.at[source],
                device_id=where,
                device_id_type=MESH,
            ),
            pltpu.make_async_remote_copy(
                src_ref=rsend_ref.at[worker],
                dst_ref=rhs_ref.at[source],
                send_sem=rsend_sem.at[worker],
                recv_sem=rrecv_sem.at[source],
                device_id=where,
                device_id_type=MESH,
            ),
        )

    @pl.when(is_worker)
    def _():
        field_ref[...] = jnp.zeros_like(field_ref)
        slot_index = lax.broadcasted_iota(jnp.int32, (1, slots), 1)
        row_iota = lax.broadcasted_iota(jnp.int32, (PATCH, slots), 0)
        col_iota = lax.broadcasted_iota(jnp.int32, (cols, slots), 0)

        @pl.loop(0, rows // PATCH)
        def _(a):
            @pl.loop(0, patch_cols)
            def _(b):
                p = a * patch_cols + b
                spot = spot_ref[pl.ds(p, 1), :]
                live = slot_index < alive_ref[p]
                spread = jnp.where(live, spread_ref[pl.ds(p, 1), :], 0.0)
                weight = spread.astype(bf16).astype(f32)
                level = spread * heat_ref[pl.ds(p, 1), :]
                parts = [weight]
                for value in (level, spread):
                    for _ in range(3):
                        part = value.astype(bf16).astype(f32)
                        parts.append(part)
                        value = value - part
                in_row = row_iota == lax.shift_right_logical(spot, 4)
                in_col = col_iota == (spot & (PATCH - 1)) + b * PATCH
                left = jnp.concatenate([jnp.where(in_row, part, 0.0) for part in parts], axis=0)
                right = jnp.where(in_col, 1.0, 0.0).astype(bf16)
                sums = lax.dot_general(left.astype(bf16), right, NT, preferred_element_type=f32)
                base = pl.multiple_of(a * PATCH, PATCH)
                for q, chosen in enumerate(((0,), (3, 2, 1), (6, 5, 4))):
                    total = field_ref[pl.ds(q * rows + base, PATCH), :]
                    for c in chosen:
                        total = total + sums[c * PATCH : (c + 1) * PATCH]
                    field_ref[pl.ds(q * rows + base, PATCH), :] = total

        for k in range(groups):
            table = field_ref[pl.ds(k * WORKERS + mine, 8, stride=rows), :]
            wsend_ref[k] = table
            wcells_ref[HALO + k] = table

        @pl.when(has_below)
        def _():
            weight_copy(1).start()

        @pl.when(has_above)
        def _():
            weight_copy(2).start()

        for k in range(groups):
            cells_ref[HALO + k, lag] = send_ref[mine, k]

        @pl.when(tile == 0)
        def _():
            cells_ref[0:HALO] = jnp.zeros((HALO, lags, share, cols), bf16)
            wcells_ref[0:HALO] = jnp.zeros((HALO, 8, cols), f32)

        @pl.when(tile == tiles - 1)
        def _():
            cells_ref[HALO + groups :] = jnp.zeros((HALO, lags, share, cols), bf16)
            wcells_ref[HALO + groups :] = jnp.zeros((HALO, 8, cols), f32)

        sub = lax.broadcasted_iota(jnp.int32, (patch_cols, cols), 0)
        lane = lax.broadcasted_iota(jnp.int32, (patch_cols, cols), 1)
        col_offset = (lane - PATCH * sub).astype(f32) - 7.5
        col_square = col_offset * col_offset
        squares = []
        for a in range(2):
            radius = jnp.zeros((patch_cols, cols), f32)
            for b in range(patch_cols):
                value = radius_ref[a * patch_cols + b].astype(f32)
                radius = jnp.where(sub == b, value, radius)
            squares.append(radius * radius)

        acc_ref[...] = jnp.zeros_like(acc_ref)
        half = patch_cols // 2

        def accumulate(jj):
            wides, anomalies, scales, weighteds = [], [], [], []
            for n in range(2):
                j = 2 * jj + n
                values = cells_ref[j].astype(f32).reshape(members, cols)
                average = jnp.sum(values, axis=0, keepdims=True) / members
                anomaly = (values - average).astype(bf16)
                anomalies.append(anomaly)
                wides.append(anomaly.astype(f32))
                table = wcells_ref[j]
                innovation = table[1:2] - table[2:3] * average
                for a in range(2):
                    row_offset = (WORKERS * j - PATCH * a - 24 + mine).astype(f32) - 7.5
                    taper = 1.0 - (row_offset * row_offset + col_square) / squares[a]
                    taper = jnp.maximum(0.0, taper)
                    taper = taper * taper
                    both = taper[:half] + taper[half:]
                    scales.append(both * table[0:1])
                    weighteds.append(both * innovation)
            for b in range(half):
                lefts, rights = [], []
                for n in range(2):
                    column = []
                    for a in range(2):
                        scale, weighted = scales[2 * n + a], weighteds[2 * n + a]
                        column.append((wides[n] * scale[b : b + 1]).astype(bf16))
                        extra = jnp.where(sub == 0, weighted[b : b + 1], 0.0)
                        extra = jnp.concatenate([extra, jnp.zeros_like(extra)], axis=0)
                        column.append(extra.astype(bf16))
                    lefts.append(jnp.concatenate(column, axis=0))
                    near = lane[:1] < PATCH * b + 40
                    near, far = (
                        jnp.where(near, 1.0, 0.0).astype(bf16),
                        jnp.where(near, 0.0, 1.0).astype(bf16),
                    )
                    rights.append(
                        jnp.concatenate([anomalies[n] * near, anomalies[n] * far], axis=0)
                    )
                left = jnp.concatenate(lefts, axis=1)
                right = jnp.concatenate(rights, axis=1)
                acc_ref[b] += lax.dot_general(left, right, NT, preferred_element_type=f32)

        for source in range(lags):

            @pl.when(source != lag)
            def _():
                sides(0, source).wait_recv()

        @pl.loop(HALO // 2, (HALO + groups) // 2)
        def _(jj):
            accumulate(jj)

        @pl.loop(0, 2)
        def _(turn):
            side = jnp.where(tile < tiles // 2, turn, 1 - turn)

            @pl.when(jnp.logical_and(side == 0, has_above))
            def _():
                for source in range(lags):
                    sides(1, source).wait_recv()
                weight_copy(1).wait_recv()

            @pl.when(jnp.logical_and(side == 1, has_below))
            def _():
                for source in range(lags):
                    sides(2, source).wait_recv()
                weight_copy(2).wait_recv()

            @pl.loop(0, HALO // 2)
            def _(n):
                accumulate(n + side * ((HALO + groups) // 2))

        for worker in range(WORKERS):
            for a in range(2):
                base = a * block_rows
                gsend_ref[worker, a] = acc_ref[worker, base : base + members].astype(bf16)
                rsend_ref[worker, a : a + 1] = acc_ref[
                    worker, base + members : base + members + 1
                ]

        for worker in range(WORKERS):

            @pl.when(worker != mine)
            def _():
                for copy in gram_copies(worker, mine):
                    copy.start()

        gram_ref[mine] = gsend_ref[mine]
        rhs_ref[mine] = rsend_ref[mine]

    row_major = lax.broadcasted_iota(jnp.int32, (share * rows, share * rows), 0)
    member_major = lax.broadcasted_iota(jnp.int32, (share * rows, share * rows), 1)
    wanted = lax.rem(row_major, share) * rows + row_major // share
    turn_ref[...] = jnp.where(member_major == wanted, 1.0, 0.0).astype(bf16)

    loads[6].wait()

    def lift(m, total):
        for n in range(8):
            total = total + hist_ref[8 * m + n].astype(f32)
        return total

    mean = lax.fori_loop(0, members // 8, lift, jnp.zeros((rows, cols), f32)) / members
    mean_ref[...] = mean

    @pl.loop(0, members // 8)
    def _(m):
        for n in range(8):
            hist_ref[8 * m + n] = (hist_ref[8 * m + n].astype(f32) - mean).astype(bf16)

    @pl.loop(0, members // (2 * share))
    def _(g):
        first = hist_ref[pl.ds(2 * share * g, share)].reshape(share * rows, cols)
        second = hist_ref[pl.ds(2 * share * g + share, share)].reshape(share * rows, cols)
        pair = jnp.concatenate([first, second], axis=1)
        turned = jnp.dot(turn_ref[...], pair, preferred_element_type=f32)
        turned = turned.reshape(rows, share, 2 * cols)
        turned = jnp.concatenate([turned[:, :, :cols], turned[:, :, cols:]], axis=1)
        start = pl.multiple_of(2 * share * g, 2 * share)
        turned_ref[:, pl.ds(start, 2 * share), :] = turned.astype(bf16)


    def transform_copy(target_lag, worker):
        return pltpu.make_async_remote_copy(
            src_ref=tsend_ref,
            dst_ref=trans_ref.at[worker],
            send_sem=tsend_sem.at[target_lag],
            recv_sem=trecv_sem.at[worker],
            device_id=place(tile, target_lag),
            device_id_type=MESH,
        )

    @pl.when(is_worker)
    def _():
        for source in range(WORKERS):

            @pl.when(source != mine)
            def _():
                for copy in gram_copies(0, source):
                    copy.wait_recv()

        identity = (
            lax.broadcasted_iota(jnp.int32, (members, members), 0)
            == lax.broadcasted_iota(jnp.int32, (members, members), 1)
        ).astype(f32)
        halves, sides_ = [], []
        for a in range(2):
            gram = gram_ref[0, a].astype(f32)
            rhs = rhs_ref[0, a : a + 1]
            for source in range(1, WORKERS):
                gram = gram + gram_ref[source, a].astype(f32)
                rhs = rhs + rhs_ref[source, a : a + 1]
            halves += [gram[:, :members], gram[:, members:]]
            sides_ += [rhs[:, :members], rhs[:, members:]]
        bounds = [
            members
            - 1.0
            + jnp.sqrt(jnp.sum(jnp.sum(x * x, axis=1, keepdims=True), axis=0, keepdims=True))
            for x in halves
        ]
        iterates = [(x + (members - 1.0) * identity) / bound for x, bound in zip(halves, bounds)]
        roots = [1.5 * identity - 0.5 * iterate for iterate in iterates]
        iterates = [product(iterate, root) for iterate, root in zip(iterates, roots)]
        for sweep in range(1, NS_STEPS):
            corrections = [
                1.5 * identity - 0.5 * product(root, iterate)
                for root, iterate in zip(roots, iterates)
            ]
            if sweep < NS_STEPS - 1:
                iterates = [product(y, c) for y, c in zip(iterates, corrections)]
            roots = [product(c, root) for c, root in zip(corrections, roots)]
        transforms = []
        for root, side, bound in zip(roots, sides_, bounds):
            inner = jnp.sum(root * side, axis=1, keepdims=True)
            weights = jnp.sum(root * inner, axis=0, keepdims=True) / bound
            factor = jnp.sqrt(jnp.full_like(bound, members - 1.0)) / jnp.sqrt(bound)
            transforms.append(factor * root + weights)
        for a in range(2):
            tsend_ref[a] = jnp.concatenate(transforms[2 * a : 2 * a + 2], axis=1).astype(bf16)

        for target in (0, lags - 1, 1, lags - 2, 2, lags - 3, 3, lags - 4):

            @pl.when(target != lag)
            def _():
                transform_copy(target, mine).start()

        trans_ref[mine] = tsend_ref[...]

    lane_patch = lax.broadcasted_iota(jnp.int32, (members, cols), 1) // PATCH
    half_rows = rows // 2

    @pl.loop(0, WORKERS)
    def _(step):
        near = jnp.where(is_worker, mine, jnp.where(lag < first, 0, WORKERS - 1))
        worker = jnp.where(
            is_worker, lax.rem(near + step, WORKERS), jnp.where(lag < first, step, near - step)
        )

        @pl.when(worker != mine)
        def _():
            transform_copy(lag, worker).wait_recv()

        mine_low = lane_patch == worker
        mine_high = lane_patch == worker + WORKERS
        mask = jnp.logical_or(mine_low, mine_high)
        low = jnp.where(mine_low[:1], 1.0, 0.0).astype(bf16)
        high = jnp.where(mine_high[:1], 1.0, 0.0).astype(bf16)
        for a in range(2):
            block = trans_ref[worker, a]

            @pl.loop(0, half_rows // 2, unroll=8)
            def _(i):
                rights = []
                for n in range(2):
                    state = turned_ref[a * half_rows + 2 * i + n]
                    rights.append(jnp.concatenate([state * low, state * high], axis=0))
                right = jnp.concatenate(rights, axis=1)
                mixed = jnp.dot(block, right, preferred_element_type=f32)
                for n in range(2):
                    r = a * half_rows + 2 * i + n
                    value = mixed[:, n * cols : (n + 1) * cols] + mean_ref[pl.ds(r, 1), :]
                    pltpu.store(mixed_ref.at[r], value, mask=mask)

    @pl.loop(0, rows, unroll=4)
    def _(r):
        out_ref[r] = mixed_ref[r].astype(bf16)

    @pl.when(has_below)
    def _():
        for worker in range(WORKERS):
            cell_copy(1, worker, lag).wait_send()

    @pl.when(has_above)
    def _():
        for worker in range(WORKERS):
            cell_copy(2, worker, lag).wait_send()

    for worker in range(WORKERS):

        @pl.when(worker != mine)
        def _():
            cell_copy(0, worker, lag).wait_send()

    @pl.when(is_worker)
    def _():
        @pl.when(has_below)
        def _():
            weight_copy(1).wait_send()

        @pl.when(has_above)
        def _():
            weight_copy(2).wait_send()

        for worker in range(WORKERS):

            @pl.when(worker != mine)
            def _():
                for copy in gram_copies(worker, mine):
                    copy.wait_send()

        for target in range(lags):

            @pl.when(target != lag)
            def _():
                transform_copy(target, mine).wait_send()


def solution(mesh):
    tiles, lags = mesh.shape["dom"], mesh.shape["lag"]

    def shards(history, forecast, spot, alive, heat, spread, radius):
        share, rows, cols = forecast.shape
        members = share * lags
        groups = rows // WORKERS
        window = groups + 2 * HALO
        f32, bf16, dma = jnp.float32, jnp.bfloat16, pltpu.SemaphoreType.DMA
        result = pl.pallas_call(
            functools.partial(kernel, tiles, lags),
            out_shape=jax.ShapeDtypeStruct((rows, members, cols), history.dtype),
            in_specs=[pl.BlockSpec(memory_space=pl.ANY)] * 7,
            out_specs=pl.BlockSpec(memory_space=pltpu.VMEM),
            scratch_shapes=[
                pltpu.VMEM(forecast.shape, bf16),
                pltpu.VMEM(spot.shape, jnp.int32),
                pltpu.VMEM(heat.shape, f32),
                pltpu.VMEM(spread.shape, f32),
                pltpu.SMEM(alive.shape, jnp.int32),
                pltpu.SMEM(radius.shape, jnp.int32),
                pltpu.VMEM((members, rows, cols), bf16),
                pltpu.VMEM((rows, members, cols), f32),
                pltpu.VMEM((share * rows, share * rows), bf16),
                pltpu.VMEM((rows, cols), f32),
                pltpu.VMEM((rows, members, cols), bf16),
                pltpu.VMEM((share * rows, cols), f32),
                pltpu.VMEM((WORKERS, groups, share, cols), bf16),
                pltpu.VMEM((window, lags, share, cols), bf16),
                pltpu.VMEM((8 * rows, cols), f32),
                pltpu.VMEM((groups, 8, cols), f32),
                pltpu.VMEM((window, 8, cols), f32),
                pltpu.VMEM((WORKERS, 2 * (members + 16), 2 * members), f32),
                pltpu.VMEM((WORKERS, 2, members, 2 * members), bf16),
                pltpu.VMEM((WORKERS, 2, members, 2 * members), bf16),
                pltpu.VMEM((WORKERS, 2, 2 * members), f32),
                pltpu.VMEM((WORKERS, 2, 2 * members), f32),
                pltpu.VMEM((2, members, 2 * members), bf16),
                pltpu.VMEM((WORKERS, 2, members, 2 * members), bf16),
                dma((7,)),
                dma((3, lags)),
                dma((3, lags)),
                dma((2,)),
                dma((2,)),
                dma((lags,)),
                dma((lags,)),
                dma((lags,)),
                dma((lags,)),
                dma((lags,)),
                dma((lags,)),
            ],
            compiler_params=pltpu.CompilerParams(collective_id=0, has_side_effects=True),
            name="smoother",
        )(forecast, spot, heat, spread, alive, radius, history)
        return jnp.transpose(result, (1, 0, 2))[None]

    in_specs = (
        P("lag", None, "dom", None),
        P("lag", "dom", None),
        P("dom", None),
        P("dom"),
        P("dom", None),
        P("dom", None),
        P("dom"),
    )
    out_specs = P("lag", None, "dom", None)
    return jax.shard_map(shards, mesh=mesh, in_specs=in_specs, out_specs=out_specs, check_vma=False)
```

time: 257 us -> 41.3 us (0.16)
  the two profiles are of different devices: /device:TPU:2 before, /device:TPU:31 now
where the time goes in v2:
time: 41.3 us; the launch traced here: 41.2 us
  Pallas kernels  39 us (94%)
  local copies, waits for them, and re-layouts  2.18 us (5%)
    pallas_call x1, Pallas kernels, shards(): pl.pallas_call(functools.partial(kernel, tiles, lags), out_shape=jax.Shap...  39 us
    broadcast_in_dim x1, local copies, waits for them, and re-layouts, shards(): return jnp.transpose(result, (1, 0, 2))[None]  2.18 us

profile of v2, /device:TPU:31, one launch (start us, length us, event | category | flops | bytes accessed | tf_op | source)
XLA Modules:
  0.0 41.2 jit_solution(8582787111089769321)
XLA Ops:
  0.0 39.0 %smoother.1 = bf16[32,64,128]{2,1,0:T(8,128)(2,1)} custom-call(bf16[8,32,128]{2,1,0:T(8,128)(2,1)} %fore_hbm.1, s32[16,256]{1,0:T(8,128)} %spot_hbm.1, f32[16,256]{1,0:T(8,128)} %heat_hbm.1, f32[16,256]{1,0:T(8,128)} %spread_hbm.1, s32[16]{0:T(128)} %alive_hbm.1, s32[16]{0:T(128)} %radius_hbm.1, bf16[1,64,32,128]{3,2,1,0:T(8,128)(2,1)} %hist_hbm.1), custom_call_target="tpu_custom_call" | custom-call | tf_op jit(solution)/shard_map/smoother/pallas_call | solution.py:575
  39.0 2.2 %copy.8 = bf16[1,64,32,128]{3,2,1,0:T(8,128)(2,1)} copy(bf16[1,64,32,128]{3,1,2,0:T(8,128)(2,1)} %bitcast.3) | data formatting | bytes 1048576 | tf_op jit(solution)/shard_map/broadcast_in_dim | solution.py:620

commit v3 on v2

--- a/solution.py
+++ b/solution.py
@@ -20,11 +20,14 @@
     return high, (x - high.astype(jnp.float32)).astype(jnp.bfloat16)
 
 
-def product(x, y):
+def product(x, y, low, high):
     xh, xl = split2(x)
     yh, yl = split2(y)
+    yh = jnp.concatenate([yh * low, yh * high], axis=0)
+    yl = jnp.concatenate([yl * low, yl * high], axis=0)
     dot = functools.partial(jnp.dot, preferred_element_type=jnp.float32)
-    return dot(xh, yh) + (dot(xh, yl) + dot(xl, yh))
+    wide = dot(jnp.concatenate([xh, xl], axis=1), jnp.concatenate([yh, yh], axis=0))
+    return wide + dot(xh, yl)
 
 
 def kernel(
@@ -281,6 +284,40 @@
             cells_ref[HALO + groups :] = jnp.zeros((HALO, lags, share, cols), bf16)
             wcells_ref[HALO + groups :] = jnp.zeros((HALO, 8, cols), f32)
 
+    row_major = lax.broadcasted_iota(jnp.int32, (share * rows, share * rows), 0)
+    member_major = lax.broadcasted_iota(jnp.int32, (share * rows, share * rows), 1)
+    wanted = lax.rem(row_major, share) * rows + row_major // share
+    turn_ref[...] = jnp.where(member_major == wanted, 1.0, 0.0).astype(bf16)
+
+    loads[6].wait()
+
+    def lift(m, total):
+        for n in range(8):
+            total = total + hist_ref[8 * m + n].astype(f32)
+        return total
+
+    mean = lax.fori_loop(0, members // 8, lift, jnp.zeros((rows, cols), f32)) / members
+    mean_ref[...] = mean
+
+    @pl.loop(0, members // 8)
+    def _(m):
+        for n in range(8):
+            hist_ref[8 * m + n] = (hist_ref[8 * m + n].astype(f32) - mean).astype(bf16)
+
+    @pl.loop(0, members // (2 * share))
+    def _(g):
+        first = hist_ref[pl.ds(2 * share * g, share)].reshape(share * rows, cols)
+        second = hist_ref[pl.ds(2 * share * g + share, share)].reshape(share * rows, cols)
+        pair = jnp.concatenate([first, second], axis=1)
+        turned = jnp.dot(turn_ref[...], pair, preferred_element_type=f32)
+        turned = turned.reshape(rows, share, 2 * cols)
+        turned = jnp.concatenate([turned[:, :, :cols], turned[:, :, cols:]], axis=1)
+        start = pl.multiple_of(2 * share * g, 2 * share)
+        turned_ref[:, pl.ds(start, 2 * share), :] = turned.astype(bf16)
+
+
+    @pl.when(is_worker)
+    def _():
         sub = lax.broadcasted_iota(jnp.int32, (patch_cols, cols), 0)
         lane = lax.broadcasted_iota(jnp.int32, (patch_cols, cols), 1)
         col_offset = (lane - PATCH * sub).astype(f32) - 7.5
@@ -296,10 +333,10 @@
         acc_ref[...] = jnp.zeros_like(acc_ref)
         half = patch_cols // 2
 
-        def accumulate(jj):
+        def accumulate(begin, count):
             wides, anomalies, scales, weighteds = [], [], [], []
-            for n in range(2):
-                j = 2 * jj + n
+            for n in range(count):
+                j = begin + n
                 values = cells_ref[j].astype(f32).reshape(members, cols)
                 average = jnp.sum(values, axis=0, keepdims=True) / members
                 anomaly = (values - average).astype(bf16)
@@ -316,8 +353,13 @@
                     scales.append(both * table[0:1])
                     weighteds.append(both * innovation)
             for b in range(half):
+                near = lane[:1] < PATCH * b + 40
+                near, far = (
+                    jnp.where(near, 1.0, 0.0).astype(bf16),
+                    jnp.where(near, 0.0, 1.0).astype(bf16),
+                )
                 lefts, rights = [], []
-                for n in range(2):
+                for n in range(count):
                     column = []
                     for a in range(2):
                         scale, weighted = scales[2 * n + a], weighteds[2 * n + a]
@@ -326,11 +368,6 @@
                         extra = jnp.concatenate([extra, jnp.zeros_like(extra)], axis=0)
                         column.append(extra.astype(bf16))
                     lefts.append(jnp.concatenate(column, axis=0))
-                    near = lane[:1] < PATCH * b + 40
-                    near, far = (
-                        jnp.where(near, 1.0, 0.0).astype(bf16),
-                        jnp.where(near, 0.0, 1.0).astype(bf16),
-                    )
                     rights.append(
                         jnp.concatenate([anomalies[n] * near, anomalies[n] * far], axis=0)
                     )
@@ -344,9 +381,9 @@
             def _():
                 sides(0, source).wait_recv()
 
-        @pl.loop(HALO // 2, (HALO + groups) // 2)
-        def _(jj):
-            accumulate(jj)
+        @pl.loop(0, 2)
+        def _(n):
+            accumulate(HALO + n * (groups // 2), groups // 2)
 
         @pl.loop(0, 2)
         def _(turn):
@@ -364,9 +401,7 @@
                     sides(2, source).wait_recv()
                 weight_copy(2).wait_recv()
 
-            @pl.loop(0, HALO // 2)
-            def _(n):
-                accumulate(n + side * ((HALO + groups) // 2))
+            accumulate(side * (HALO + groups), HALO)
 
         for worker in range(WORKERS):
             for a in range(2):
@@ -385,38 +420,6 @@
 
         gram_ref[mine] = gsend_ref[mine]
         rhs_ref[mine] = rsend_ref[mine]
-
-    row_major = lax.broadcasted_iota(jnp.int32, (share * rows, share * rows), 0)
-    member_major = lax.broadcasted_iota(jnp.int32, (share * rows, share * rows), 1)
-    wanted = lax.rem(row_major, share) * rows + row_major // share
-    turn_ref[...] = jnp.where(member_major == wanted, 1.0, 0.0).astype(bf16)
-
-    loads[6].wait()
-
-    def lift(m, total):
-        for n in range(8):
-            total = total + hist_ref[8 * m + n].astype(f32)
-        return total
-
-    mean = lax.fori_loop(0, members // 8, lift, jnp.zeros((rows, cols), f32)) / members
-    mean_ref[...] = mean
-
-    @pl.loop(0, members // 8)
-    def _(m):
-        for n in range(8):
-            hist_ref[8 * m + n] = (hist_ref[8 * m + n].astype(f32) - mean).astype(bf16)
-
-    @pl.loop(0, members // (2 * share))
-    def _(g):
-        first = hist_ref[pl.ds(2 * share * g, share)].reshape(share * rows, cols)
-        second = hist_ref[pl.ds(2 * share * g + share, share)].reshape(share * rows, cols)
-        pair = jnp.concatenate([first, second], axis=1)
-        turned = jnp.dot(turn_ref[...], pair, preferred_element_type=f32)
-        turned = turned.reshape(rows, share, 2 * cols)
-        turned = jnp.concatenate([turned[:, :, :cols], turned[:, :, cols:]], axis=1)
-        start = pl.multiple_of(2 * share * g, 2 * share)
-        turned_ref[:, pl.ds(start, 2 * share), :] = turned.astype(bf16)
-
 
     def transform_copy(target_lag, worker):
         return pltpu.make_async_remote_copy(
@@ -437,44 +440,50 @@
                 for copy in gram_copies(0, source):
                     copy.wait_recv()
 
-        identity = (
-            lax.broadcasted_iota(jnp.int32, (members, members), 0)
-            == lax.broadcasted_iota(jnp.int32, (members, members), 1)
-        ).astype(f32)
-        halves, sides_ = [], []
+        row = lax.broadcasted_iota(jnp.int32, (members, 2 * members), 0)
+        column = lax.broadcasted_iota(jnp.int32, (members, 2 * members), 1)
+        identity = (row == lax.rem(column, members)).astype(f32)
+        is_low = column[:1] < members
+        low = jnp.where(is_low, 1.0, 0.0).astype(bf16)
+        high = jnp.where(is_low, 0.0, 1.0).astype(bf16)
+
+        def pick(values):
+            return jnp.where(is_low, values[0], values[1])
+
+        def lane_sums(x):
+            return [
+                jnp.sum(x[:, n * members : (n + 1) * members], axis=1, keepdims=True)
+                for n in range(2)
+            ]
+
+        iterates, roots, bounds, rights_ = [], [], [], []
         for a in range(2):
             gram = gram_ref[0, a].astype(f32)
             rhs = rhs_ref[0, a : a + 1]
             for source in range(1, WORKERS):
                 gram = gram + gram_ref[source, a].astype(f32)
                 rhs = rhs + rhs_ref[source, a : a + 1]
-            halves += [gram[:, :members], gram[:, members:]]
-            sides_ += [rhs[:, :members], rhs[:, members:]]
-        bounds = [
-            members
-            - 1.0
-            + jnp.sqrt(jnp.sum(jnp.sum(x * x, axis=1, keepdims=True), axis=0, keepdims=True))
-            for x in halves
-        ]
-        iterates = [(x + (members - 1.0) * identity) / bound for x, bound in zip(halves, bounds)]
+            squares_ = lane_sums(jnp.sum(gram * gram, axis=0, keepdims=True))
+            bound = members - 1.0 + jnp.sqrt(pick(squares_))
+            bounds.append(bound)
+            rights_.append(rhs)
+            iterates.append((gram + (members - 1.0) * identity) / bound)
         roots = [1.5 * identity - 0.5 * iterate for iterate in iterates]
-        iterates = [product(iterate, root) for iterate, root in zip(iterates, roots)]
+        iterates = [product(y, root, low, high) for y, root in zip(iterates, roots)]
         for sweep in range(1, NS_STEPS):
             corrections = [
-                1.5 * identity - 0.5 * product(root, iterate)
-                for root, iterate in zip(roots, iterates)
+                1.5 * identity - 0.5 * product(root, y, low, high)
+                for root, y in zip(roots, iterates)
             ]
             if sweep < NS_STEPS - 1:
-                iterates = [product(y, c) for y, c in zip(iterates, corrections)]
-            roots = [product(c, root) for c, root in zip(corrections, roots)]
-        transforms = []
-        for root, side, bound in zip(roots, sides_, bounds):
-            inner = jnp.sum(root * side, axis=1, keepdims=True)
+                iterates = [product(y, c, low, high) for y, c in zip(iterates, corrections)]
+            roots = [product(c, root, low, high) for c, root in zip(corrections, roots)]
+        for a in range(2):
+            root, bound = roots[a], bounds[a]
+            inner = pick(lane_sums(root * rights_[a]))
             weights = jnp.sum(root * inner, axis=0, keepdims=True) / bound
             factor = jnp.sqrt(jnp.full_like(bound, members - 1.0)) / jnp.sqrt(bound)
-            transforms.append(factor * root + weights)
-        for a in range(2):
-            tsend_ref[a] = jnp.concatenate(transforms[2 * a : 2 * a + 2], axis=1).astype(bf16)
+            tsend_ref[a] = (factor * root + weights).astype(bf16)
 
         for target in (0, lags - 1, 1, lags - 2, 2, lags - 3, 3, lags - 4):
 
@@ -575,7 +584,7 @@
         result = pl.pallas_call(
             functools.partial(kernel, tiles, lags),
             out_shape=jax.ShapeDtypeStruct((rows, members, cols), history.dtype),
-            in_specs=[pl.BlockSpec(memory_space=pl.ANY)] * 7,
+            in_specs=[pl.BlockSpec(memory_space=pltpu.HBM)] * 7,
             out_specs=pl.BlockSpec(memory_space=pltpu.VMEM),
             scratch_shapes=[
                 pltpu.VMEM(forecast.shape, bf16),
@@ -614,9 +623,16 @@
                 dma((lags,)),
                 dma((lags,)),
             ],
-            compiler_params=pltpu.CompilerParams(collective_id=0, has_side_effects=True),
+            compiler_params=pltpu.CompilerParams(
+                collective_id=0, has_side_effects=True, vmem_limit_bytes=16 << 20
+            ),
             name="smoother",
-        )(forecast, spot, heat, spread, alive, radius, history)
+        )(
+            *(
+                pltpu.with_memory_space_constraint(x, pltpu.HBM)
+                for x in (forecast, spot, heat, spread, alive, radius, history)
+            )
+        )
         return jnp.transpose(result, (1, 0, 2))[None]
 
     in_specs = (

time: 41.3 us -> 39.1 us (0.947)
  Pallas kernels: 39 us -> 37.9 us
  local copies, waits for them, and re-layouts: 2.18 us -> 1.14 us
    pallas_call x1, Pallas kernels: 39 us -> 37.9 us  [shards(): pl.pallas_call(functools.partial(kernel, tiles, lags), out_shape=jax.Shap...]
    broadcast_in_dim x1, local copies, waits for them, and re-layouts: 2.18 us -> 1.14 us  [shards(): return jnp.transpose(result, (1, 0, 2))[None]]
where the time goes in v3:
time: 39.1 us; the launch traced here: 39 us
  Pallas kernels  37.9 us (97%)
  local copies, waits for them, and re-layouts  1.14 us (3%)
    pallas_call x1, Pallas kernels, shards(): pl.pallas_call(functools.partial(kernel, tiles, lags), out_shape=jax.Shap...  37.9 us
    broadcast_in_dim x1, local copies, waits for them, and re-layouts, shards(): return jnp.transpose(result, (1, 0, 2))[None]  1.14 us

profile of v3, /device:TPU:31, one launch (start us, length us, event | category | flops | bytes accessed | tf_op | source)
XLA Modules:
  0.0 39.0 jit_solution(5147396983383261137)
XLA Ops:
  0.0 37.9 %smoother.1 = bf16[32,64,128]{2,1,0:T(8,128)(2,1)S(1)} custom-call(bf16[8,32,128]{2,1,0:T(8,128)(2,1)} %fore_hbm.1, s32[16,256]{1,0:T(8,128)} %spot_hbm.1, f32[16,256]{1,0:T(8,128)} %heat_hbm.1, f32[16,256]{1,0:T(8,128)} %spread_hbm.1, s32[16]{0:T(128)} %alive_hbm.1, s32[16]{0:T(128)} %radius_hbm.1, bf16[1,64,32,128]{3,2,1,0:T(8,128)(2,1)} %hist_hbm.1), custom_call_target="tpu_custom_call" | custom-call | tf_op jit(solution)/shard_map/smoother/pallas_call | solution.py:584
  37.9 1.1 %copy.8 = bf16[1,64,32,128]{3,2,1,0:T(8,128)(2,1)} copy(bf16[1,64,32,128]{3,1,2,0:T(8,128)(2,1)S(1)} %bitcast.3) | data formatting | bytes 1048576 | tf_op jit(solution)/shard_map/broadcast_in_dim | solution.py:636

commit v4 on v3

--- a/solution.py
+++ b/solution.py
@@ -65,6 +65,8 @@
     rhs_ref,
     tsend_ref,
     trans_ref,
+    relay_ref,
+    wrelay_ref,
     load_sem,
     send_sem,
     recv_sem,
@@ -76,6 +78,10 @@
     rrecv_sem,
     tsend_sem,
     trecv_sem,
+    hsend_sem,
+    hrecv_sem,
+    relay_sem,
+    forward_sem,
 ):
     tile = lax.axis_index("dom")
     lag = lax.axis_index("lag")
@@ -89,6 +95,12 @@
     f32, bf16 = jnp.float32, jnp.bfloat16
     has_below = tile < tiles - 1
     has_above = tile > 0
+    seam = tiles // 2
+    is_lower = tile == seam - 1
+    is_upper = tile == seam
+    is_relay = tile == tiles - 1
+    near_below = jnp.logical_and(has_below, tile != seam - 1)
+    near_above = jnp.logical_and(has_above, tile != seam)
     mine = lag - first
     is_worker = jnp.logical_and(mine >= 0, mine < WORKERS)
 
@@ -119,18 +131,30 @@
 
     @pl.when(is_worker)
     def _():
-        @pl.when(has_above)
+        @pl.when(is_lower)
+        def _():
+            for target in range(lags):
+                greet(tiles - 1, target)
+
+        @pl.when(is_upper)
         def _():
             for target in range(lags):
                 greet(tile - 1, target)
 
-        @pl.when(has_below)
-        def _():
-            for target in range(lags):
-                greet(tile + 1, target)
-
         for step in range(1, lags):
             greet(tile, lax.rem(lag + step, lags))
+
+        @pl.when(near_above)
+        def _():
+            greet(tile - 1, lag)
+
+        @pl.when(near_below)
+        def _():
+            greet(tile + 1, lag)
+
+    @pl.when(is_relay)
+    def _():
+        greet(seam, lag)
 
     for load in loads:
         load.start()
@@ -147,8 +171,11 @@
         barrier,
         WORKERS
         - jnp.where(is_worker, 1, 0)
-        + jnp.where(has_above, WORKERS, 0)
-        + jnp.where(has_below, WORKERS, 0),
+        + jnp.where(jnp.logical_and(is_worker, near_above), 1, 0)
+        + jnp.where(jnp.logical_and(is_worker, near_below), 1, 0)
+        + jnp.where(is_lower, WORKERS, 0)
+        + jnp.where(is_upper, 1, 0)
+        + jnp.where(is_relay, WORKERS, 0),
     )
 
     def cell_copy(kind, worker, source_lag):
@@ -179,15 +206,64 @@
     def order(step):
         return jnp.where(lag < lags // 2, WORKERS - 1 - step, step)
 
-    @pl.when(has_below)
+    def halo_copy(kind):
+        return pltpu.make_async_remote_copy(
+            src_ref=cells_ref.at[pl.ds(groups if kind == 1 else HALO, HALO)],
+            dst_ref=cells_ref.at[pl.ds(0 if kind == 1 else HALO + groups, HALO)],
+            send_sem=hsend_sem.at[kind - 1],
+            recv_sem=hrecv_sem.at[kind - 1],
+            device_id=place(tile + (0, 1, -1)[kind], lag),
+            device_id_type=MESH,
+        )
+
+    def relay_copy():
+        return pltpu.make_async_remote_copy(
+            src_ref=send_ref.at[:, pl.ds(0, HALO)],
+            dst_ref=relay_ref,
+            send_sem=relay_sem.at[0],
+            recv_sem=relay_sem.at[1],
+            device_id=place(tiles - 1, lag),
+            device_id_type=MESH,
+        )
+
+    def relay_weights():
+        return pltpu.make_async_remote_copy(
+            src_ref=wsend_ref.at[pl.ds(0, HALO)],
+            dst_ref=wrelay_ref,
+            send_sem=relay_sem.at[2],
+            recv_sem=relay_sem.at[3],
+            device_id=place(tiles - 1, lag),
+            device_id_type=MESH,
+        )
+
+    def forward_copy(worker):
+        return pltpu.make_async_remote_copy(
+            src_ref=relay_ref.at[worker],
+            dst_ref=cells_ref.at[pl.ds(HALO + groups, HALO), lag],
+            send_sem=forward_sem.at[worker],
+            recv_sem=recv_sem.at[2, lag],
+            device_id=place(seam - 1, first + worker),
+            device_id_type=MESH,
+        )
+
+    def forward_weights():
+        return pltpu.make_async_remote_copy(
+            src_ref=wrelay_ref,
+            dst_ref=wcells_ref.at[pl.ds(HALO + groups, HALO)],
+            send_sem=forward_sem.at[WORKERS],
+            recv_sem=wrecv_sem.at[1],
+            device_id=place(seam - 1, lag),
+            device_id_type=MESH,
+        )
+
+    @pl.when(is_lower)
     def _():
         for step in range(WORKERS):
             cell_copy(1, order(step), lag).start()
 
-    @pl.when(has_above)
-    def _():
-        for step in range(WORKERS):
-            cell_copy(2, order(step), lag).start()
+    @pl.when(is_upper)
+    def _():
+        relay_copy().start()
 
     for step in range(WORKERS):
         worker = order(step)
@@ -195,6 +271,12 @@
         @pl.when(worker != mine)
         def _():
             cell_copy(0, worker, lag).start()
+
+    @pl.when(is_relay)
+    def _():
+        relay_copy().wait_recv()
+        for step in range(WORKERS):
+            forward_copy(order(step)).start()
 
     for load in loads[1:6]:
         load.wait()
@@ -267,9 +349,18 @@
         def _():
             weight_copy(1).start()
 
-        @pl.when(has_above)
+        @pl.when(near_above)
         def _():
             weight_copy(2).start()
+
+        @pl.when(is_upper)
+        def _():
+            relay_weights().start()
+
+        @pl.when(is_relay)
+        def _():
+            relay_weights().wait_recv()
+            forward_weights().start()
 
         for k in range(groups):
             cells_ref[HALO + k, lag] = send_ref[mine, k]
@@ -381,6 +472,14 @@
             def _():
                 sides(0, source).wait_recv()
 
+        @pl.when(near_below)
+        def _():
+            halo_copy(1).start()
+
+        @pl.when(near_above)
+        def _():
+            halo_copy(2).start()
+
         @pl.loop(0, 2)
         def _(n):
             accumulate(HALO + n * (groups // 2), groups // 2)
@@ -389,16 +488,30 @@
         def _(turn):
             side = jnp.where(tile < tiles // 2, turn, 1 - turn)
 
-            @pl.when(jnp.logical_and(side == 0, has_above))
+            @pl.when(jnp.logical_and(side == 0, near_above))
+            def _():
+                halo_copy(1).wait_recv()
+
+            @pl.when(jnp.logical_and(side == 0, is_upper))
             def _():
                 for source in range(lags):
                     sides(1, source).wait_recv()
+
+            @pl.when(jnp.logical_and(side == 0, has_above))
+            def _():
                 weight_copy(1).wait_recv()
 
-            @pl.when(jnp.logical_and(side == 1, has_below))
+            @pl.when(jnp.logical_and(side == 1, near_below))
+            def _():
+                halo_copy(2).wait_recv()
+
+            @pl.when(jnp.logical_and(side == 1, is_lower))
             def _():
                 for source in range(lags):
                     sides(2, source).wait_recv()
+
+            @pl.when(jnp.logical_and(side == 1, has_below))
+            def _():
                 weight_copy(2).wait_recv()
 
             accumulate(side * (HALO + groups), HALO)
@@ -532,15 +645,19 @@
     def _(r):
         out_ref[r] = mixed_ref[r].astype(bf16)
 
-    @pl.when(has_below)
+    @pl.when(is_lower)
     def _():
         for worker in range(WORKERS):
             cell_copy(1, worker, lag).wait_send()
 
-    @pl.when(has_above)
+    @pl.when(is_upper)
+    def _():
+        relay_copy().wait_send()
+
+    @pl.when(is_relay)
     def _():
         for worker in range(WORKERS):
-            cell_copy(2, worker, lag).wait_send()
+            forward_copy(worker).wait_send()
 
     for worker in range(WORKERS):
 
@@ -554,9 +671,22 @@
         def _():
             weight_copy(1).wait_send()
 
-        @pl.when(has_above)
+        @pl.when(near_above)
         def _():
             weight_copy(2).wait_send()
+            halo_copy(2).wait_send()
+
+        @pl.when(near_below)
+        def _():
+            halo_copy(1).wait_send()
+
+        @pl.when(is_upper)
+        def _():
+            relay_weights().wait_send()
+
+        @pl.when(is_relay)
+        def _():
+            forward_weights().wait_send()
 
         for worker in range(WORKERS):
 
@@ -611,6 +741,8 @@
                 pltpu.VMEM((WORKERS, 2, 2 * members), f32),
                 pltpu.VMEM((2, members, 2 * members), bf16),
                 pltpu.VMEM((WORKERS, 2, members, 2 * members), bf16),
+                pltpu.VMEM((WORKERS, HALO, share, cols), bf16),
+                pltpu.VMEM((HALO, 8, cols), f32),
                 dma((7,)),
                 dma((3, lags)),
                 dma((3, lags)),
@@ -622,6 +754,10 @@
                 dma((lags,)),
                 dma((lags,)),
                 dma((lags,)),
+                dma((2,)),
+                dma((2,)),
+                dma((4,)),
+                dma((WORKERS + 1,)),
             ],
             compiler_params=pltpu.CompilerParams(
                 collective_id=0, has_side_effects=True, vmem_limit_bytes=16 << 20

time: 39.1 us -> 39.2 us (level)
  no operation moved by 1% of the time
where the time goes in v4:
time: 39.2 us; the launch traced here: 39 us
  Pallas kernels  37.9 us (97%)
  local copies, waits for them, and re-layouts  1.14 us (3%)
    pallas_call x1, Pallas kernels, shards(): pl.pallas_call(functools.partial(kernel, tiles, lags), out_shape=jax.Shap...  37.9 us
    broadcast_in_dim x1, local copies, waits for them, and re-layouts, shards(): return jnp.transpose(result, (1, 0, 2))[None]  1.14 us

profile of v4, /device:TPU:31, one launch (start us, length us, event | category | flops | bytes accessed | tf_op | source)
XLA Modules:
  0.0 39.0 jit_solution(14098741575845360535)
XLA Ops:
  0.0 37.9 %smoother.1 = bf16[32,64,128]{2,1,0:T(8,128)(2,1)S(1)} custom-call(bf16[8,32,128]{2,1,0:T(8,128)(2,1)} %fore_hbm.1, s32[16,256]{1,0:T(8,128)} %spot_hbm.1, f32[16,256]{1,0:T(8,128)} %heat_hbm.1, f32[16,256]{1,0:T(8,128)} %spread_hbm.1, s32[16]{0:T(128)} %alive_hbm.1, s32[16]{0:T(128)} %radius_hbm.1, bf16[1,64,32,128]{3,2,1,0:T(8,128)(2,1)} %hist_hbm.1), custom_call_target="tpu_custom_call" | custom-call | tf_op jit(solution)/shard_map/smoother/pallas_call | solution.py:714
  37.9 1.1 %copy.8 = bf16[1,64,32,128]{3,2,1,0:T(8,128)(2,1)} copy(bf16[1,64,32,128]{3,1,2,0:T(8,128)(2,1)S(1)} %bitcast.3) | data formatting | bytes 1048576 | tf_op jit(solution)/shard_map/broadcast_in_dim | solution.py:772

commit v5 on v4

--- a/solution.py
+++ b/solution.py
@@ -48,7 +48,6 @@
     alive_ref,
     radius_ref,
     hist_ref,
-    mixed_ref,
     turn_ref,
     mean_ref,
     turned_ref,
@@ -67,6 +66,8 @@
     trans_ref,
     relay_ref,
     wrelay_ref,
+    down_ref,
+    wdown_ref,
     load_sem,
     send_sem,
     recv_sem,
@@ -82,6 +83,8 @@
     hrecv_sem,
     relay_sem,
     forward_sem,
+    down_sem,
+    onward_sem,
 ):
     tile = lax.axis_index("dom")
     lag = lax.axis_index("lag")
@@ -98,7 +101,12 @@
     seam = tiles // 2
     is_lower = tile == seam - 1
     is_upper = tile == seam
-    is_relay = tile == tiles - 1
+    is_last = tile == tiles - 1
+    at_seam = jnp.logical_or(is_lower, is_upper)
+    middle = lags // 2
+    is_end = jnp.logical_and(is_last, jnp.logical_or(lag == 0, lag == lags - 1))
+    end_lag = jnp.where(lag < middle, lags - 1, 0)
+    end_base = jnp.where(lag == 0, middle, 0)
     near_below = jnp.logical_and(has_below, tile != seam - 1)
     near_above = jnp.logical_and(has_above, tile != seam)
     mine = lag - first
@@ -138,8 +146,8 @@
 
         @pl.when(is_upper)
         def _():
-            for target in range(lags):
-                greet(tile - 1, target)
+            greet(tiles - 1, 0)
+            greet(tiles - 1, lags - 1)
 
         for step in range(1, lags):
             greet(tile, lax.rem(lag + step, lags))
@@ -152,9 +160,14 @@
         def _():
             greet(tile + 1, lag)
 
-    @pl.when(is_relay)
+    @pl.when(is_last)
     def _():
         greet(seam, lag)
+
+    @pl.when(is_end)
+    def _():
+        for n in range(middle):
+            greet(seam - 1, end_base + n)
 
     for load in loads:
         load.start()
@@ -167,146 +180,10 @@
             row = k * WORKERS + target
             send_ref[target, k] = fore32_ref[pl.ds(row, share, stride=rows), :].astype(bf16)
 
-    pl.semaphore_wait(
-        barrier,
-        WORKERS
-        - jnp.where(is_worker, 1, 0)
-        + jnp.where(jnp.logical_and(is_worker, near_above), 1, 0)
-        + jnp.where(jnp.logical_and(is_worker, near_below), 1, 0)
-        + jnp.where(is_lower, WORKERS, 0)
-        + jnp.where(is_upper, 1, 0)
-        + jnp.where(is_relay, WORKERS, 0),
-    )
-
-    def cell_copy(kind, worker, source_lag):
-        begin = groups - HALO if kind == 1 else 0
-        count = groups if kind == 0 else HALO
-        start = (HALO, 0, HALO + groups)[kind]
-        return pltpu.make_async_remote_copy(
-            src_ref=send_ref.at[worker, pl.ds(begin, count)],
-            dst_ref=cells_ref.at[pl.ds(start, count), source_lag],
-            send_sem=send_sem.at[kind, worker],
-            recv_sem=recv_sem.at[kind, source_lag],
-            device_id=place(tile + (0, 1, -1)[kind], first + worker),
-            device_id_type=MESH,
-        )
-
-    def weight_copy(kind):
-        begin = groups - HALO if kind == 1 else 0
-        start = (HALO, 0, HALO + groups)[kind]
-        return pltpu.make_async_remote_copy(
-            src_ref=wsend_ref.at[pl.ds(begin, HALO)],
-            dst_ref=wcells_ref.at[pl.ds(start, HALO)],
-            send_sem=wsend_sem.at[kind - 1],
-            recv_sem=wrecv_sem.at[kind - 1],
-            device_id=place(tile + (0, 1, -1)[kind], lag),
-            device_id_type=MESH,
-        )
-
-    def order(step):
-        return jnp.where(lag < lags // 2, WORKERS - 1 - step, step)
-
-    def halo_copy(kind):
-        return pltpu.make_async_remote_copy(
-            src_ref=cells_ref.at[pl.ds(groups if kind == 1 else HALO, HALO)],
-            dst_ref=cells_ref.at[pl.ds(0 if kind == 1 else HALO + groups, HALO)],
-            send_sem=hsend_sem.at[kind - 1],
-            recv_sem=hrecv_sem.at[kind - 1],
-            device_id=place(tile + (0, 1, -1)[kind], lag),
-            device_id_type=MESH,
-        )
-
-    def relay_copy():
-        return pltpu.make_async_remote_copy(
-            src_ref=send_ref.at[:, pl.ds(0, HALO)],
-            dst_ref=relay_ref,
-            send_sem=relay_sem.at[0],
-            recv_sem=relay_sem.at[1],
-            device_id=place(tiles - 1, lag),
-            device_id_type=MESH,
-        )
-
-    def relay_weights():
-        return pltpu.make_async_remote_copy(
-            src_ref=wsend_ref.at[pl.ds(0, HALO)],
-            dst_ref=wrelay_ref,
-            send_sem=relay_sem.at[2],
-            recv_sem=relay_sem.at[3],
-            device_id=place(tiles - 1, lag),
-            device_id_type=MESH,
-        )
-
-    def forward_copy(worker):
-        return pltpu.make_async_remote_copy(
-            src_ref=relay_ref.at[worker],
-            dst_ref=cells_ref.at[pl.ds(HALO + groups, HALO), lag],
-            send_sem=forward_sem.at[worker],
-            recv_sem=recv_sem.at[2, lag],
-            device_id=place(seam - 1, first + worker),
-            device_id_type=MESH,
-        )
-
-    def forward_weights():
-        return pltpu.make_async_remote_copy(
-            src_ref=wrelay_ref,
-            dst_ref=wcells_ref.at[pl.ds(HALO + groups, HALO)],
-            send_sem=forward_sem.at[WORKERS],
-            recv_sem=wrecv_sem.at[1],
-            device_id=place(seam - 1, lag),
-            device_id_type=MESH,
-        )
-
-    @pl.when(is_lower)
-    def _():
-        for step in range(WORKERS):
-            cell_copy(1, order(step), lag).start()
-
-    @pl.when(is_upper)
-    def _():
-        relay_copy().start()
-
-    for step in range(WORKERS):
-        worker = order(step)
-
-        @pl.when(worker != mine)
-        def _():
-            cell_copy(0, worker, lag).start()
-
-    @pl.when(is_relay)
-    def _():
-        relay_copy().wait_recv()
-        for step in range(WORKERS):
-            forward_copy(order(step)).start()
-
-    for load in loads[1:6]:
-        load.wait()
-
-    def sides(kind, source_lag):
-        return cell_copy(kind, 0, source_lag)
-
-    def gram_copies(worker, source):
-        where = place(tile, first + worker)
-        return (
-            pltpu.make_async_remote_copy(
-                src_ref=gsend_ref.at[worker],
-                dst_ref=gram_ref.at[source],
-                send_sem=gsend_sem.at[worker],
-                recv_sem=grecv_sem.at[source],
-                device_id=where,
-                device_id_type=MESH,
-            ),
-            pltpu.make_async_remote_copy(
-                src_ref=rsend_ref.at[worker],
-                dst_ref=rhs_ref.at[source],
-                send_sem=rsend_sem.at[worker],
-                recv_sem=rrecv_sem.at[source],
-                device_id=where,
-                device_id_type=MESH,
-            ),
-        )
-
-    @pl.when(is_worker)
-    def _():
+    def weight_sums():
+        for load in loads[1:6]:
+            load.wait()
+
         field_ref[...] = jnp.zeros_like(field_ref)
         slot_index = lax.broadcasted_iota(jnp.int32, (1, slots), 1)
         row_iota = lax.broadcasted_iota(jnp.int32, (PATCH, slots), 0)
@@ -345,7 +222,190 @@
             wsend_ref[k] = table
             wcells_ref[HALO + k] = table
 
-        @pl.when(has_below)
+    @pl.when(jnp.logical_and(is_worker, at_seam))
+    def _():
+        weight_sums()
+
+    pl.semaphore_wait(
+        barrier,
+        WORKERS
+        - jnp.where(is_worker, 1, 0)
+        + jnp.where(jnp.logical_and(is_worker, near_above), 1, 0)
+        + jnp.where(jnp.logical_and(is_worker, near_below), 1, 0)
+        + jnp.where(at_seam, 1, 0)
+        + jnp.where(is_last, WORKERS, 0)
+        + jnp.where(is_end, WORKERS, 0),
+    )
+
+    def cell_copy(kind, worker, source_lag):
+        begin = groups - HALO if kind == 1 else 0
+        count = groups if kind == 0 else HALO
+        start = (HALO, 0, HALO + groups)[kind]
+        return pltpu.make_async_remote_copy(
+            src_ref=send_ref.at[worker, pl.ds(begin, count)],
+            dst_ref=cells_ref.at[pl.ds(start, count), source_lag],
+            send_sem=send_sem.at[kind, worker],
+            recv_sem=recv_sem.at[kind, source_lag],
+            device_id=place(tile + (0, 1, -1)[kind], first + worker),
+            device_id_type=MESH,
+        )
+
+    def weight_copy(kind):
+        begin = groups - HALO if kind == 1 else 0
+        start = (HALO, 0, HALO + groups)[kind]
+        return pltpu.make_async_remote_copy(
+            src_ref=wsend_ref.at[pl.ds(begin, HALO)],
+            dst_ref=wcells_ref.at[pl.ds(start, HALO)],
+            send_sem=wsend_sem.at[kind - 1],
+            recv_sem=wrecv_sem.at[kind - 1],
+            device_id=place(tile + (0, 1, -1)[kind], lag),
+            device_id_type=MESH,
+        )
+
+    def order(step):
+        return jnp.where(lag < lags // 2, WORKERS - 1 - step, step)
+
+    def halo_copy(kind):
+        return pltpu.make_async_remote_copy(
+            src_ref=cells_ref.at[pl.ds(groups if kind == 1 else HALO, HALO)],
+            dst_ref=cells_ref.at[pl.ds(0 if kind == 1 else HALO + groups, HALO)],
+            send_sem=hsend_sem.at[kind - 1],
+            recv_sem=hrecv_sem.at[kind - 1],
+            device_id=place(tile + (0, 1, -1)[kind], lag),
+            device_id_type=MESH,
+        )
+
+    def up_copy():
+        return pltpu.make_async_remote_copy(
+            src_ref=send_ref.at[:, pl.ds(0, HALO)],
+            dst_ref=relay_ref,
+            send_sem=relay_sem.at[0],
+            recv_sem=relay_sem.at[1],
+            device_id=place(tiles - 1, lag),
+            device_id_type=MESH,
+        )
+
+    def up_weights():
+        return pltpu.make_async_remote_copy(
+            src_ref=wsend_ref.at[pl.ds(0, HALO)],
+            dst_ref=wrelay_ref,
+            send_sem=relay_sem.at[2],
+            recv_sem=relay_sem.at[3],
+            device_id=place(tiles - 1, lag),
+            device_id_type=MESH,
+        )
+
+    def up_forward(worker):
+        return pltpu.make_async_remote_copy(
+            src_ref=relay_ref.at[worker],
+            dst_ref=cells_ref.at[pl.ds(HALO + groups, HALO), lag],
+            send_sem=forward_sem.at[worker],
+            recv_sem=recv_sem.at[2, lag],
+            device_id=place(seam - 1, first + worker),
+            device_id_type=MESH,
+        )
+
+    def up_forward_weights():
+        return pltpu.make_async_remote_copy(
+            src_ref=wrelay_ref,
+            dst_ref=wcells_ref.at[pl.ds(HALO + groups, HALO)],
+            send_sem=forward_sem.at[WORKERS],
+            recv_sem=wrecv_sem.at[1],
+            device_id=place(seam - 1, lag),
+            device_id_type=MESH,
+        )
+
+    def down_copy(source):
+        return pltpu.make_async_remote_copy(
+            src_ref=send_ref.at[:, pl.ds(groups - HALO, HALO)],
+            dst_ref=down_ref.at[source],
+            send_sem=relay_sem.at[0],
+            recv_sem=down_sem.at[0, source],
+            device_id=place(tiles - 1, end_lag),
+            device_id_type=MESH,
+        )
+
+    def down_weights(source):
+        return pltpu.make_async_remote_copy(
+            src_ref=wsend_ref.at[pl.ds(groups - HALO, HALO)],
+            dst_ref=wdown_ref.at[source],
+            send_sem=relay_sem.at[2],
+            recv_sem=down_sem.at[1, source],
+            device_id=place(tiles - 1, end_lag),
+            device_id_type=MESH,
+        )
+
+    def down_forward(source, worker):
+        return pltpu.make_async_remote_copy(
+            src_ref=down_ref.at[source, worker],
+            dst_ref=cells_ref.at[pl.ds(0, HALO), source],
+            send_sem=onward_sem.at[source, worker],
+            recv_sem=recv_sem.at[1, source],
+            device_id=place(seam, first + worker),
+            device_id_type=MESH,
+        )
+
+    def down_forward_weights(source):
+        return pltpu.make_async_remote_copy(
+            src_ref=wdown_ref.at[source],
+            dst_ref=wcells_ref.at[pl.ds(0, HALO)],
+            send_sem=onward_sem.at[source, WORKERS],
+            recv_sem=wrecv_sem.at[0],
+            device_id=place(seam, source),
+            device_id_type=MESH,
+        )
+
+    @pl.when(is_lower)
+    def _():
+        down_copy(lag).start()
+
+    @pl.when(is_upper)
+    def _():
+        up_copy().start()
+
+    for step in range(WORKERS):
+        worker = order(step)
+
+        @pl.when(worker != mine)
+        def _():
+            cell_copy(0, worker, lag).start()
+
+    def sides(kind, source_lag):
+        return cell_copy(kind, 0, source_lag)
+
+    def gram_copies(worker, source):
+        where = place(tile, first + worker)
+        return (
+            pltpu.make_async_remote_copy(
+                src_ref=gsend_ref.at[worker],
+                dst_ref=gram_ref.at[source],
+                send_sem=gsend_sem.at[worker],
+                recv_sem=grecv_sem.at[source],
+                device_id=where,
+                device_id_type=MESH,
+            ),
+            pltpu.make_async_remote_copy(
+                src_ref=rsend_ref.at[worker],
+                dst_ref=rhs_ref.at[source],
+                send_sem=rsend_sem.at[worker],
+                recv_sem=rrecv_sem.at[source],
+                device_id=where,
+                device_id_type=MESH,
+            ),
+        )
+
+    @pl.when(jnp.logical_and(is_worker, jnp.logical_not(at_seam)))
+    def _():
+        weight_sums()
+
+    @pl.when(jnp.logical_not(is_worker))
+    def _():
+        for load in loads[1:6]:
+            load.wait()
+
+    @pl.when(is_worker)
+    def _():
+        @pl.when(near_below)
         def _():
             weight_copy(1).start()
 
@@ -353,14 +413,13 @@
         def _():
             weight_copy(2).start()
 
+        @pl.when(is_lower)
+        def _():
+            down_weights(lag).start()
+
         @pl.when(is_upper)
         def _():
-            relay_weights().start()
-
-        @pl.when(is_relay)
-        def _():
-            relay_weights().wait_recv()
-            forward_weights().start()
+            up_weights().start()
 
         for k in range(groups):
             cells_ref[HALO + k, lag] = send_ref[mine, k]
@@ -374,11 +433,43 @@
         def _():
             cells_ref[HALO + groups :] = jnp.zeros((HALO, lags, share, cols), bf16)
             wcells_ref[HALO + groups :] = jnp.zeros((HALO, 8, cols), f32)
+
+    @pl.when(is_last)
+    def _():
+        up_copy().wait_recv()
+        for step in range(WORKERS):
+            up_forward(order(step)).start()
+
+        @pl.when(is_worker)
+        def _():
+            up_weights().wait_recv()
+            up_forward_weights().start()
+
+    def sends_weights(source):
+        return jnp.logical_and(source >= first, source < first + WORKERS)
+
+    @pl.when(is_end)
+    def _():
+        @pl.loop(0, middle)
+        def _(n):
+            source = end_base + n
+            down_copy(source).wait_recv()
+            for worker in range(WORKERS):
+                down_forward(source, worker).start()
+
+            @pl.when(sends_weights(source))
+            def _():
+                down_weights(source).wait_recv()
+                down_forward_weights(source).start()
 
     row_major = lax.broadcasted_iota(jnp.int32, (share * rows, share * rows), 0)
     member_major = lax.broadcasted_iota(jnp.int32, (share * rows, share * rows), 1)
     wanted = lax.rem(row_major, share) * rows + row_major // share
     turn_ref[...] = jnp.where(member_major == wanted, 1.0, 0.0).astype(bf16)
+
+    @pl.loop(0, rows)
+    def _(r):
+        out_ref[r] = jnp.zeros((members, cols), bf16)
 
     loads[6].wait()
 
@@ -639,25 +730,44 @@
                 for n in range(2):
                     r = a * half_rows + 2 * i + n
                     value = mixed[:, n * cols : (n + 1) * cols] + mean_ref[pl.ds(r, 1), :]
-                    pltpu.store(mixed_ref.at[r], value, mask=mask)
-
-    @pl.loop(0, rows, unroll=4)
-    def _(r):
-        out_ref[r] = mixed_ref[r].astype(bf16)
+                    out_ref[r] = jnp.where(mask, value.astype(bf16), out_ref[r])
 
     @pl.when(is_lower)
     def _():
+        down_copy(lag).wait_send()
+
+        @pl.when(is_worker)
+        def _():
+            down_weights(lag).wait_send()
+
+    @pl.when(is_upper)
+    def _():
+        up_copy().wait_send()
+
+        @pl.when(is_worker)
+        def _():
+            up_weights().wait_send()
+
+    @pl.when(is_last)
+    def _():
         for worker in range(WORKERS):
-            cell_copy(1, worker, lag).wait_send()
-
-    @pl.when(is_upper)
-    def _():
-        relay_copy().wait_send()
-
-    @pl.when(is_relay)
-    def _():
-        for worker in range(WORKERS):
-            forward_copy(worker).wait_send()
+            up_forward(worker).wait_send()
+
+        @pl.when(is_worker)
+        def _():
+            up_forward_weights().wait_send()
+
+    @pl.when(is_end)
+    def _():
+        @pl.loop(0, middle)
+        def _(n):
+            source = end_base + n
+            for worker in range(WORKERS):
+                down_forward(source, worker).wait_send()
+
+            @pl.when(sends_weights(source))
+            def _():
+                down_forward_weights(source).wait_send()
 
     for worker in range(WORKERS):
 
@@ -667,10 +777,6 @@
 
     @pl.when(is_worker)
     def _():
-        @pl.when(has_below)
-        def _():
-            weight_copy(1).wait_send()
-
         @pl.when(near_above)
         def _():
             weight_copy(2).wait_send()
@@ -678,15 +784,8 @@
 
         @pl.when(near_below)
         def _():
+            weight_copy(1).wait_send()
             halo_copy(1).wait_send()
-
-        @pl.when(is_upper)
-        def _():
-            relay_weights().wait_send()
-
-        @pl.when(is_relay)
-        def _():
-            forward_weights().wait_send()
 
         for worker in range(WORKERS):
 
@@ -724,7 +823,6 @@
                 pltpu.SMEM(alive.shape, jnp.int32),
                 pltpu.SMEM(radius.shape, jnp.int32),
                 pltpu.VMEM((members, rows, cols), bf16),
-                pltpu.VMEM((rows, members, cols), f32),
                 pltpu.VMEM((share * rows, share * rows), bf16),
                 pltpu.VMEM((rows, cols), f32),
                 pltpu.VMEM((rows, members, cols), bf16),
@@ -743,6 +841,8 @@
                 pltpu.VMEM((WORKERS, 2, members, 2 * members), bf16),
                 pltpu.VMEM((WORKERS, HALO, share, cols), bf16),
                 pltpu.VMEM((HALO, 8, cols), f32),
+                pltpu.VMEM((lags, WORKERS, HALO, share, cols), bf16),
+                pltpu.VMEM((lags, HALO, 8, cols), f32),
                 dma((7,)),
                 dma((3, lags)),
                 dma((3, lags)),
@@ -758,6 +858,8 @@
                 dma((2,)),
                 dma((4,)),
                 dma((WORKERS + 1,)),
+                dma((2, lags)),
+                dma((lags, WORKERS + 1)),
             ],
             compiler_params=pltpu.CompilerParams(
                 collective_id=0, has_side_effects=True, vmem_limit_bytes=16 << 20

time: 39.2 us -> 38 us (0.969)
  Pallas kernels: 37.9 us -> 36.8 us
    pallas_call x1, Pallas kernels: 37.9 us -> 36.8 us  [shards(): pl.pallas_call(functools.partial(kernel, tiles, lags), out_shape=jax.Shap...]
where the time goes in v5:
time: 38 us; the launch traced here: 37.9 us
  Pallas kernels  36.8 us (97%)
  local copies, waits for them, and re-layouts  1.14 us (3%)
    pallas_call x1, Pallas kernels, shards(): pl.pallas_call(functools.partial(kernel, tiles, lags), out_shape=jax.Shap...  36.8 us
    broadcast_in_dim x1, local copies, waits for them, and re-layouts, shards(): return jnp.transpose(result, (1, 0, 2))[None]  1.14 us

profile of v5, /device:TPU:31, one launch (start us, length us, event | category | flops | bytes accessed | tf_op | source)
XLA Modules:
  0.0 37.9 jit_solution(3011811326106036356)
XLA Ops:
  0.0 36.8 %smoother.1 = bf16[32,64,128]{2,1,0:T(8,128)(2,1)S(1)} custom-call(bf16[8,32,128]{2,1,0:T(8,128)(2,1)} %fore_hbm.1, s32[16,256]{1,0:T(8,128)} %spot_hbm.1, f32[16,256]{1,0:T(8,128)} %heat_hbm.1, f32[16,256]{1,0:T(8,128)} %spread_hbm.1, s32[16]{0:T(128)} %alive_hbm.1, s32[16]{0:T(128)} %radius_hbm.1, bf16[1,64,32,128]{3,2,1,0:T(8,128)(2,1)} %hist_hbm.1), custom_call_target="tpu_custom_call" | custom-call | tf_op jit(solution)/shard_map/smoother/pallas_call | solution.py:813
  36.8 1.1 %copy.8 = bf16[1,64,32,128]{3,2,1,0:T(8,128)(2,1)} copy(bf16[1,64,32,128]{3,1,2,0:T(8,128)(2,1)S(1)} %bitcast.3) | data formatting | bytes 1048576 | tf_op jit(solution)/shard_map/broadcast_in_dim | solution.py:874

commit v6 on v5

--- a/solution.py
+++ b/solution.py
@@ -58,6 +58,7 @@
     wsend_ref,
     wcells_ref,
     acc_ref,
+    accw_ref,
     gsend_ref,
     gram_ref,
     rsend_ref,
@@ -93,7 +94,6 @@
     groups = rows // WORKERS
     patch_cols = cols // PATCH
     slots = spot_ref.shape[1]
-    block_rows = members + 16
     first = lags // 2 - WORKERS // 2
     f32, bf16 = jnp.float32, jnp.bfloat16
     has_below = tile < tiles - 1
@@ -244,8 +244,8 @@
         return pltpu.make_async_remote_copy(
             src_ref=send_ref.at[worker, pl.ds(begin, count)],
             dst_ref=cells_ref.at[pl.ds(start, count), source_lag],
-            send_sem=send_sem.at[kind, worker],
-            recv_sem=recv_sem.at[kind, source_lag],
+            send_sem=send_sem.at[worker],
+            recv_sem=recv_sem.at[min(kind, 1)],
             device_id=place(tile + (0, 1, -1)[kind], first + worker),
             device_id_type=MESH,
         )
@@ -299,8 +299,8 @@
         return pltpu.make_async_remote_copy(
             src_ref=relay_ref.at[worker],
             dst_ref=cells_ref.at[pl.ds(HALO + groups, HALO), lag],
-            send_sem=forward_sem.at[worker],
-            recv_sem=recv_sem.at[2, lag],
+            send_sem=forward_sem.at[0],
+            recv_sem=recv_sem.at[1],
             device_id=place(seam - 1, first + worker),
             device_id_type=MESH,
         )
@@ -309,7 +309,7 @@
         return pltpu.make_async_remote_copy(
             src_ref=wrelay_ref,
             dst_ref=wcells_ref.at[pl.ds(HALO + groups, HALO)],
-            send_sem=forward_sem.at[WORKERS],
+            send_sem=forward_sem.at[1],
             recv_sem=wrecv_sem.at[1],
             device_id=place(seam - 1, lag),
             device_id_type=MESH,
@@ -320,7 +320,7 @@
             src_ref=send_ref.at[:, pl.ds(groups - HALO, HALO)],
             dst_ref=down_ref.at[source],
             send_sem=relay_sem.at[0],
-            recv_sem=down_sem.at[0, source],
+            recv_sem=down_sem.at[0, lax.rem(source, lags // 2)],
             device_id=place(tiles - 1, end_lag),
             device_id_type=MESH,
         )
@@ -330,7 +330,7 @@
             src_ref=wsend_ref.at[pl.ds(groups - HALO, HALO)],
             dst_ref=wdown_ref.at[source],
             send_sem=relay_sem.at[2],
-            recv_sem=down_sem.at[1, source],
+            recv_sem=down_sem.at[1, lax.rem(source, lags // 2)],
             device_id=place(tiles - 1, end_lag),
             device_id_type=MESH,
         )
@@ -339,8 +339,8 @@
         return pltpu.make_async_remote_copy(
             src_ref=down_ref.at[source, worker],
             dst_ref=cells_ref.at[pl.ds(0, HALO), source],
-            send_sem=onward_sem.at[source, worker],
-            recv_sem=recv_sem.at[1, source],
+            send_sem=onward_sem.at[0, lax.rem(source, lags // 2)],
+            recv_sem=recv_sem.at[1],
             device_id=place(seam, first + worker),
             device_id_type=MESH,
         )
@@ -349,7 +349,7 @@
         return pltpu.make_async_remote_copy(
             src_ref=wdown_ref.at[source],
             dst_ref=wcells_ref.at[pl.ds(0, HALO)],
-            send_sem=onward_sem.at[source, WORKERS],
+            send_sem=onward_sem.at[1, lax.rem(source, lags // 2)],
             recv_sem=wrecv_sem.at[0],
             device_id=place(seam, source),
             device_id_type=MESH,
@@ -370,8 +370,11 @@
         def _():
             cell_copy(0, worker, lag).start()
 
-    def sides(kind, source_lag):
-        return cell_copy(kind, 0, source_lag)
+    def arrived(kind):
+        block = cells_ref.at[
+            pl.ds((HALO, 0, HALO + groups)[kind], groups if kind == 0 else HALO)
+        ]
+        return pltpu.make_async_copy(block, block, recv_sem.at[min(kind, 1)])
 
     def gram_copies(worker, source):
         where = place(tile, first + worker)
@@ -421,8 +424,9 @@
         def _():
             up_weights().start()
 
-        for k in range(groups):
-            cells_ref[HALO + k, lag] = send_ref[mine, k]
+        pltpu.make_async_copy(
+            send_ref.at[mine], cells_ref.at[pl.ds(HALO, groups), lag], recv_sem.at[0]
+        ).start()
 
         @pl.when(tile == 0)
         def _():
@@ -513,6 +517,7 @@
             squares.append(radius * radius)
 
         acc_ref[...] = jnp.zeros_like(acc_ref)
+        accw_ref[...] = jnp.zeros_like(accw_ref)
         half = patch_cols // 2
 
         def accumulate(begin, count):
@@ -533,35 +538,33 @@
                     taper = taper * taper
                     both = taper[:half] + taper[half:]
                     scales.append(both * table[0:1])
-                    weighteds.append(both * innovation)
+                    weighteds.append(taper * innovation)
+            left = jnp.concatenate(anomalies, axis=1)
             for b in range(half):
                 near = lane[:1] < PATCH * b + 40
                 near, far = (
                     jnp.where(near, 1.0, 0.0).astype(bf16),
                     jnp.where(near, 0.0, 1.0).astype(bf16),
                 )
-                lefts, rights = [], []
+                rights = []
                 for n in range(count):
                     column = []
                     for a in range(2):
-                        scale, weighted = scales[2 * n + a], weighteds[2 * n + a]
-                        column.append((wides[n] * scale[b : b + 1]).astype(bf16))
-                        extra = jnp.where(sub == 0, weighted[b : b + 1], 0.0)
-                        extra = jnp.concatenate([extra, jnp.zeros_like(extra)], axis=0)
-                        column.append(extra.astype(bf16))
-                    lefts.append(jnp.concatenate(column, axis=0))
-                    rights.append(
-                        jnp.concatenate([anomalies[n] * near, anomalies[n] * far], axis=0)
-                    )
-                left = jnp.concatenate(lefts, axis=1)
+                        scaled = (wides[n] * scales[2 * n + a][b : b + 1]).astype(bf16)
+                        column += [scaled * near, scaled * far]
+                    rights.append(jnp.concatenate(column, axis=0))
                 right = jnp.concatenate(rights, axis=1)
                 acc_ref[b] += lax.dot_general(left, right, NT, preferred_element_type=f32)
-
-        for source in range(lags):
-
-            @pl.when(source != lag)
-            def _():
-                sides(0, source).wait_recv()
+            side_left = jnp.concatenate(
+                [
+                    jnp.concatenate(weighteds[2 * n : 2 * n + 2], axis=0).astype(bf16)
+                    for n in range(count)
+                ],
+                axis=1,
+            )
+            accw_ref[...] += lax.dot_general(side_left, left, NT, preferred_element_type=f32)
+
+        arrived(0).wait()
 
         @pl.when(near_below)
         def _():
@@ -585,8 +588,7 @@
 
             @pl.when(jnp.logical_and(side == 0, is_upper))
             def _():
-                for source in range(lags):
-                    sides(1, source).wait_recv()
+                arrived(1).wait()
 
             @pl.when(jnp.logical_and(side == 0, has_above))
             def _():
@@ -598,8 +600,7 @@
 
             @pl.when(jnp.logical_and(side == 1, is_lower))
             def _():
-                for source in range(lags):
-                    sides(2, source).wait_recv()
+                arrived(2).wait()
 
             @pl.when(jnp.logical_and(side == 1, has_below))
             def _():
@@ -609,11 +610,12 @@
 
         for worker in range(WORKERS):
             for a in range(2):
-                base = a * block_rows
-                gsend_ref[worker, a] = acc_ref[worker, base : base + members].astype(bf16)
-                rsend_ref[worker, a : a + 1] = acc_ref[
-                    worker, base + members : base + members + 1
-                ]
+                lanes = slice(2 * a * members, 2 * (a + 1) * members)
+                gsend_ref[worker, a] = acc_ref[worker, :, lanes].astype(bf16)
+                q = a * patch_cols + worker
+                rsend_ref[worker, a : a + 1] = jnp.concatenate(
+                    [accw_ref[q : q + 1], accw_ref[q + half : q + half + 1]], axis=1
+                )
 
         for worker in range(WORKERS):
 
@@ -750,8 +752,7 @@
 
     @pl.when(is_last)
     def _():
-        for worker in range(WORKERS):
-            up_forward(worker).wait_send()
+        pltpu.make_async_copy(relay_ref, relay_ref, forward_sem.at[0]).wait()
 
         @pl.when(is_worker)
         def _():
@@ -762,8 +763,9 @@
         @pl.loop(0, middle)
         def _(n):
             source = end_base + n
-            for worker in range(WORKERS):
-                down_forward(source, worker).wait_send()
+            pltpu.make_async_copy(
+                down_ref.at[source], down_ref.at[source], onward_sem.at[0, n]
+            ).wait()
 
             @pl.when(sends_weights(source))
             def _():
@@ -832,7 +834,8 @@
                 pltpu.VMEM((8 * rows, cols), f32),
                 pltpu.VMEM((groups, 8, cols), f32),
                 pltpu.VMEM((window, 8, cols), f32),
-                pltpu.VMEM((WORKERS, 2 * (members + 16), 2 * members), f32),
+                pltpu.VMEM((WORKERS, members, 4 * members), f32),
+                pltpu.VMEM((2 * WORKERS * 2, members), f32),
                 pltpu.VMEM((WORKERS, 2, members, 2 * members), bf16),
                 pltpu.VMEM((WORKERS, 2, members, 2 * members), bf16),
                 pltpu.VMEM((WORKERS, 2, 2 * members), f32),
@@ -844,22 +847,22 @@
                 pltpu.VMEM((lags, WORKERS, HALO, share, cols), bf16),
                 pltpu.VMEM((lags, HALO, 8, cols), f32),
                 dma((7,)),
-                dma((3, lags)),
-                dma((3, lags)),
+                dma((WORKERS,)),
                 dma((2,)),
                 dma((2,)),
+                dma((2,)),
+                dma((WORKERS,)),
+                dma((WORKERS,)),
+                dma((WORKERS,)),
+                dma((WORKERS,)),
                 dma((lags,)),
-                dma((lags,)),
-                dma((lags,)),
-                dma((lags,)),
-                dma((lags,)),
-                dma((lags,)),
+                dma((WORKERS,)),
                 dma((2,)),
                 dma((2,)),
                 dma((4,)),
-                dma((WORKERS + 1,)),
-                dma((2, lags)),
-                dma((lags, WORKERS + 1)),
+                dma((2,)),
+                dma((2, lags // 2)),
+                dma((2, lags // 2)),
             ],
             compiler_params=pltpu.CompilerParams(
                 collective_id=0, has_side_effects=True, vmem_limit_bytes=16 << 20

time: 38 us -> 36.5 us (0.961)
  the two profiles are of different devices: /device:TPU:31 before, /device:TPU:448 now
where the time goes in v6:
time: 36.5 us; the launch traced here: 36.4 us
  Pallas kernels  35.2 us (96%)
  local copies, waits for them, and re-layouts  1.14 us (3%)
    pallas_call x1, Pallas kernels, shards(): pl.pallas_call(functools.partial(kernel, tiles, lags), out_shape=jax.Shap...  35.2 us
    broadcast_in_dim x1, local copies, waits for them, and re-layouts, shards(): return jnp.transpose(result, (1, 0, 2))[None]  1.14 us

profile of v6, /device:TPU:448, one launch (start us, length us, event | category | flops | bytes accessed | tf_op | source)
XLA Modules:
  0.0 36.4 jit_solution(10931910207915883731)
XLA Ops:
  0.0 35.2 %smoother.1 = bf16[32,64,128]{2,1,0:T(8,128)(2,1)S(1)} custom-call(bf16[8,32,128]{2,1,0:T(8,128)(2,1)} %fore_hbm.1, s32[16,256]{1,0:T(8,128)} %spot_hbm.1, f32[16,256]{1,0:T(8,128)} %heat_hbm.1, f32[16,256]{1,0:T(8,128)} %spread_hbm.1, s32[16]{0:T(128)} %alive_hbm.1, s32[16]{0:T(128)} %radius_hbm.1, bf16[1,64,32,128]{3,2,1,0:T(8,128)(2,1)} %hist_hbm.1), custom_call_target="tpu_custom_call" | custom-call | tf_op jit(solution)/shard_map/smoother/pallas_call | solution.py:815
  35.2 1.1 %copy.8 = bf16[1,64,32,128]{3,2,1,0:T(8,128)(2,1)} copy(bf16[1,64,32,128]{3,1,2,0:T(8,128)(2,1)S(1)} %bitcast.3) | data formatting | bytes 1048576 | tf_op jit(solution)/shard_map/broadcast_in_dim | solution.py:877

commit v7 on v6

--- a/solution.py
+++ b/solution.py
@@ -103,6 +103,7 @@
     is_upper = tile == seam
     is_last = tile == tiles - 1
     at_seam = jnp.logical_or(is_lower, is_upper)
+    sums_early = jnp.logical_or(at_seam, is_last)
     middle = lags // 2
     is_end = jnp.logical_and(is_last, jnp.logical_or(lag == 0, lag == lags - 1))
     end_lag = jnp.where(lag < middle, lags - 1, 0)
@@ -222,7 +223,7 @@
             wsend_ref[k] = table
             wcells_ref[HALO + k] = table
 
-    @pl.when(jnp.logical_and(is_worker, at_seam))
+    @pl.when(jnp.logical_and(is_worker, sums_early))
     def _():
         weight_sums()
 
@@ -397,7 +398,7 @@
             ),
         )
 
-    @pl.when(jnp.logical_and(is_worker, jnp.logical_not(at_seam)))
+    @pl.when(jnp.logical_and(is_worker, jnp.logical_not(sums_early)))
     def _():
         weight_sums()
 

time: 36.5 us -> 36.6 us (level)
  no operation moved by 1% of the time
where the time goes in v7:
time: 36.6 us; the launch traced here: 36.5 us
  Pallas kernels  35.3 us (96%)
  local copies, waits for them, and re-layouts  1.14 us (3%)
    pallas_call x1, Pallas kernels, shards(): pl.pallas_call(functools.partial(kernel, tiles, lags), out_shape=jax.Shap...  35.3 us
    broadcast_in_dim x1, local copies, waits for them, and re-layouts, shards(): return jnp.transpose(result, (1, 0, 2))[None]  1.14 us

profile of v7, /device:TPU:448, one launch (start us, length us, event | category | flops | bytes accessed | tf_op | source)
XLA Modules:
  0.0 36.5 jit_solution(7678073201718072918)
XLA Ops:
  0.0 35.3 %smoother.1 = bf16[32,64,128]{2,1,0:T(8,128)(2,1)S(1)} custom-call(bf16[8,32,128]{2,1,0:T(8,128)(2,1)} %fore_hbm.1, s32[16,256]{1,0:T(8,128)} %spot_hbm.1, f32[16,256]{1,0:T(8,128)} %heat_hbm.1, f32[16,256]{1,0:T(8,128)} %spread_hbm.1, s32[16]{0:T(128)} %alive_hbm.1, s32[16]{0:T(128)} %radius_hbm.1, bf16[1,64,32,128]{3,2,1,0:T(8,128)(2,1)} %hist_hbm.1), custom_call_target="tpu_custom_call" | custom-call | tf_op jit(solution)/shard_map/smoother/pallas_call | solution.py:816
  35.3 1.1 %copy.8 = bf16[1,64,32,128]{3,2,1,0:T(8,128)(2,1)} copy(bf16[1,64,32,128]{3,1,2,0:T(8,128)(2,1)S(1)} %bitcast.3) | data formatting | bytes 1048576 | tf_op jit(solution)/shard_map/broadcast_in_dim | solution.py:878

commit v8 on v7

--- a/solution.py
+++ b/solution.py
@@ -462,6 +462,10 @@
             for worker in range(WORKERS):
                 down_forward(source, worker).start()
 
+        @pl.loop(0, middle)
+        def _(n):
+            source = end_base + n
+
             @pl.when(sends_weights(source))
             def _():
                 down_weights(source).wait_recv()

time: 36.6 us -> 36.2 us (0.989)
  the two profiles are of different devices: /device:TPU:448 before, /device:TPU:31 now
where the time goes in v8:
time: 36.2 us; the launch traced here: 36.1 us
  Pallas kernels  35 us (97%)
  local copies, waits for them, and re-layouts  1.14 us (3%)
    pallas_call x1, Pallas kernels, shards(): pl.pallas_call(functools.partial(kernel, tiles, lags), out_shape=jax.Shap...  35 us
    broadcast_in_dim x1, local copies, waits for them, and re-layouts, shards(): return jnp.transpose(result, (1, 0, 2))[None]  1.14 us

profile of v8, /device:TPU:31, one launch (start us, length us, event | category | flops | bytes accessed | tf_op | source)
XLA Modules:
  0.0 36.1 jit_solution(1027637585569121164)
XLA Ops:
  0.0 35.0 %smoother.1 = bf16[32,64,128]{2,1,0:T(8,128)(2,1)S(1)} custom-call(bf16[8,32,128]{2,1,0:T(8,128)(2,1)} %fore_hbm.1, s32[16,256]{1,0:T(8,128)} %spot_hbm.1, f32[16,256]{1,0:T(8,128)} %heat_hbm.1, f32[16,256]{1,0:T(8,128)} %spread_hbm.1, s32[16]{0:T(128)} %alive_hbm.1, s32[16]{0:T(128)} %radius_hbm.1, bf16[1,64,32,128]{3,2,1,0:T(8,128)(2,1)} %hist_hbm.1), custom_call_target="tpu_custom_call" | custom-call | tf_op jit(solution)/shard_map/smoother/pallas_call | solution.py:820
  35.0 1.1 %copy.8 = bf16[1,64,32,128]{3,2,1,0:T(8,128)(2,1)} copy(bf16[1,64,32,128]{3,1,2,0:T(8,128)(2,1)S(1)} %bitcast.3) | data formatting | bytes 1048576 | tf_op jit(solution)/shard_map/broadcast_in_dim | solution.py:882
